TPU v7x, 256 devices: a whole 4x4x8 slice. The times are simulated.
256 devices in a mesh: row: 8 (over z_lo, x), col: 32 (over y, z_hi, core).
Axes of the slice: x: 4, y: 4, z: 8 (z_hi: 4, z_lo: 2; z = z_hi * 2 + z_lo), core: 2. Of those that a mesh axis runs over, the one named last changes fastest.
Arguments:
- features: float32 [8192, 256], P(('row', 'col')), may hold values from -4 to 4
- neighbors: int32 [8192, 10], P(('row', 'col')), may hold values from 0 to 8191
- pivot: int32 [1], replicated, may hold values from 0 to 31
Outputs:
- distances: float32 [8192, 8192], P('row', 'col')
Inputs may be any that keep to these rules, and one draw needn't show every extreme that they name: `neighbors`: point indices; a list may repeat an index or name its own point. The pivot block holds the points pivot[0] * 256 onward.
All inputs are finite; a program needn't handle non-finite values.
Results may differ from a plain program's by a relative error of at most 0.00005.
Values sent between devices are 32-bit elements; how exact they have to be, the bound alone decides.
A program may use at most 64 MiB of HBM per device.

v0:
```python
import jax
import jax.numpy as jnp
from jax import lax
from jax.sharding import PartitionSpec as P

PB = 256
SQUARINGS = 3


far_weight = 3.0


def copy_for_each(value, axis):
    size = lax.axis_size(axis)
    return lax.all_to_all(
        jnp.broadcast_to(value[None], (size, *value.shape)), axis, 0, 0, tiled=True
    )


def joined_along(pieces, dim):
    dims = list(pieces.shape[1:])
    dims[dim] *= pieces.shape[0]
    return jnp.moveaxis(pieces, 0, dim).reshape(dims)


def collect(value, axis, dim):
    pieces = copy_for_each(value, axis)
    return joined_along(pieces, dim)


def picked(value, axis, root):
    return lax.dynamic_index_in_dim(lax.all_gather(value, axis), root, 0, keepdims=False)


def weights_of(points_a, lists_a, ids_a, points_b, lists_b, ids_b):
    norm_a = jnp.sum(points_a * points_a, axis=1)
    norm_b = jnp.sum(points_b * points_b, axis=1)
    inner = jnp.einsum("if,jf->ij", points_a, points_b, precision=lax.Precision.HIGHEST)
    squares = norm_a[:, None] + norm_b[None, :] - 2.0 * inner
    length = jnp.sqrt(jnp.maximum(squares, 0.0))
    linked = jnp.zeros(squares.shape, dtype=bool)
    for slot in range(lists_a.shape[1]):
        linked = linked | (lists_a[:, slot][:, None] == ids_b[None, :])
        linked = linked | (lists_b[:, slot][None, :] == ids_a[:, None])
    weighted = jnp.where(linked, length, far_weight * length)
    return jnp.where(ids_a[:, None] == ids_b[None, :], jnp.zeros_like(weighted), weighted)


def min_plus(left, right):
    inner_width = left.shape[1]
    step = min(64, inner_width)
    best = None
    for start in range(0, inner_width, step):
        piece = jnp.min(
            left[:, start : start + step, None] + right[None, start : start + step, :], axis=1
        )
        best = piece if best is None else jnp.minimum(best, piece)
    return best


def close_block(block):
    for turn in range(SQUARINGS):
        block = jnp.minimum(block, min_plus(block, block))
    return block


def local(features, neighbors, pivot):
    row_points, row_lists = (collect(features, "col", 0), collect(neighbors, "col", 0))
    row_count = row_points.shape[0]
    col_count = row_count * lax.axis_size("row") // lax.axis_size("col")
    row_index = lax.axis_index("row")
    col_index = lax.axis_index("col")
    offset = jnp.clip(col_index * col_count - row_index * row_count, 0, row_count - col_count)
    col_points = lax.dynamic_slice_in_dim(row_points, offset, col_count, 0)
    col_lists = lax.dynamic_slice_in_dim(row_lists, offset, col_count, 0)
    owner_row = col_index * col_count // row_count
    col_points, col_lists = (
        picked(col_points, "row", owner_row),
        picked(col_lists, "row", owner_row),
    )
    row_ids = row_index * row_count + jnp.arange(row_count, dtype=jnp.int32)
    col_ids = col_index * col_count + jnp.arange(col_count, dtype=jnp.int32)
    tile = weights_of(row_points, row_lists, row_ids, col_points, col_lists, col_ids)
    pivot_base = pivot[0] * PB
    pivot_row = pivot_base // row_count
    row_offset = jnp.clip(pivot_base - row_index * row_count, 0, row_count - PB)
    pivot_feats = lax.dynamic_slice_in_dim(row_points, row_offset, PB, 0)
    pivot_lists = lax.dynamic_slice_in_dim(row_lists, row_offset, PB, 0)
    pivot_feats, pivot_lists = (
        picked(pivot_feats, "row", pivot_row),
        picked(pivot_lists, "row", pivot_row),
    )
    pivot_ids = pivot_base + jnp.arange(PB, dtype=jnp.int32)
    closed = close_block(
        weights_of(pivot_feats, pivot_lists, pivot_ids, pivot_feats, pivot_lists, pivot_ids)
    )
    row_raw = weights_of(pivot_feats, pivot_lists, pivot_ids, col_points, col_lists, col_ids)
    col_raw = weights_of(row_points, row_lists, row_ids, pivot_feats, pivot_lists, pivot_ids)
    row_panel = jnp.minimum(row_raw, min_plus(closed, row_raw))
    col_panel = jnp.minimum(col_raw, min_plus(col_raw, closed))
    return jnp.minimum(tile, min_plus(col_panel, row_panel))


def solution(mesh):
    return jax.shard_map(
        local,
        mesh=mesh,
        in_specs=(P(("row", "col"), None), P(("row", "col"), None), P()),
        out_specs=P("row", "col"),
        check_vma=False,
    )
```

profile of v0, /device:TPU:6, one launch (start us, length us, event | category | flops | bytes accessed | tf_op | source)
XLA Modules:
  0.0 612.3 jit_solution(3587835970071700755)
XLA Ops:
  6.5 1.9 broadcast_in_dim.5
  8.4 11.5 %all-to-all-start.1 = ((f32[32,32,256]{2,1,0:T(8,128)}), f32[32,32,256]{2,1,0:T(8,128)S(1)}, u32[]{:S(2)}, u32[]{:S(2)}) async-start(f32[32,32,256]{2,1,0:T(8,128)} %broadcast_in_dim.5), calls=%async_computation.1 | async-start | bytes 2097152 | tf_op jit(solution)/shard_map/all_to_all | solution.py:15
  20.6 29.0 %all-to-all-done.1 = f32[32,32,256]{2,1,0:T(8,128)S(1)} async-done(((f32[32,32,256]{2,1,0:T(8,128)}), f32[32,32,256]{2,1,0:T(8,128)S(1)}, u32[]{:S(2)}, u32[]{:S(2)}) %all-to-all-start.1) | async-done | bytes 1048608 | tf_op jit(solution)/shard_map/all_to_all | solution.py:15
  49.6 0.8 constant_dynamic-slice_fusion
  50.5 0.8 reshape.106
  51.2 3.9 all-to-all-start
  55.2 9.7 %all-to-all-done = s32[32,1,320]{2,1,0:T(1,128)S(1)} async-done(((s32[32,1,320]{2,1,0:T(1,128)}), s32[32,1,320]{2,1,0:T(1,128)S(1)}, u32[]{:S(2)}, u32[]{:S(2)}) %all-to-all-start) | async-done | bytes 40992 | tf_op jit(solution)/shard_map/all_to_all | solution.py:15
  65.0 0.5 broadcast.110
  65.5 0.7 reduce.1
  66.6 28.2 %all-gather.2 = s32[2048,10]{0,1:T(8,128)S(1)} all-gather(s32[256,10]{0,1:T(8,128)S(1)} %get-tuple-element.65), channel_id=4, replica_groups=mesh['row'=8,'col'=32] {'row'}, dimensions={0}, use_global_device_ids=true | all-gather | bytes 92160 | tf_op jit(solution)/shard_map/all_gather | solution.py:32
  95.0 28.2 %all-gather = s32[2048,10]{0,1:T(8,128)S(1)} all-gather(s32[256,10]{0,1:T(8,128)S(1)} %get-tuple-element.66), channel_id=2, replica_groups=mesh['row'=8,'col'=32] {'row'}, dimensions={0}, use_global_device_ids=true | all-gather | bytes 92160 | tf_op jit(solution)/shard_map/all_gather | solution.py:32
  123.5 0.2 multiply_reduce_fusion
  123.8 1.1 fusion.22
  124.9 2.9 fusion.18
  127.8 0.1 fusion.45
  127.9 4.8 add_reduce_fusion.22
  132.8 4.8 add_reduce_fusion.20
  137.6 4.8 add_reduce_fusion.21
  142.4 4.8 add_reduce_fusion.23
  147.4 4.8 add_reduce_fusion.18
  152.2 4.8 add_reduce_fusion.16
  157.0 4.8 add_reduce_fusion.17
  161.8 4.8 add_reduce_fusion.19
  166.9 4.8 add_reduce_fusion.14
  171.7 4.8 add_reduce_fusion.12
  176.5 5.0 add_reduce_fusion.13
  181.5 4.8 add_reduce_fusion.15
  186.4 0.7 fusion.38
  187.2 1.1 fusion.25
  188.4 2.3 fusion.17
  190.8 4.8 add_reduce_fusion.10
  195.6 4.8 add_reduce_fusion.8
  200.4 4.8 add_reduce_fusion.9
  205.2 4.8 add_reduce_fusion.11
  210.1 0.7 fusion.37
  210.8 4.7 fusion.4
  215.6 0.9 fusion.36
  216.5 1.0 copy.48
  217.5 45.9 %add_reduce_fusion.6 = f32[1024,256]{1,0:T(8,128)S(1)} fusion(f32[64,256]{1,0:T(8,128)} %get-tuple-element.19, f32[1024,64]{1,0:T(8,128)} %copy.48), kind=kLoop, calls=%fused_computation.6 | loop fusion | flops 33292288 | bytes 1376256 | tf_op jit(solution)/shard_map/reduce_min | solution.py:54
  263.4 1.3 copy.50
  264.7 1.9 copy.53
  266.6 45.7 %add_reduce_fusion.4 = f32[1024,256]{1,0:T(8,128)S(1)} fusion(f32[64,256]{1,0:T(8,128)} %get-tuple-element.20, f32[1024,64]{1,0:T(8,128)} %copy.53), kind=kLoop, calls=%fused_computation.4 | loop fusion | flops 33292288 | bytes 1376256 | tf_op jit(solution)/shard_map/reduce_min | solution.py:54
  312.3 1.3 copy.54
  313.6 1.9 copy.51
  315.6 45.7 %add_reduce_fusion.5 = f32[1024,256]{1,0:T(8,128)S(1)} fusion(f32[64,256]{1,0:T(8,128)} %get-tuple-element.21, f32[1024,64]{1,0:T(8,128)} %copy.51), kind=kLoop, calls=%fused_computation.5 | loop fusion | flops 33292288 | bytes 1376256 | tf_op jit(solution)/shard_map/reduce_min | solution.py:54
  361.3 1.3 copy.52
  362.6 1.0 copy.47
  363.6 45.8 %add_reduce_fusion.7 = f32[1024,256]{1,0:T(8,128)S(1)} fusion(f32[64,256]{1,0:T(8,128)S(1)} %get-tuple-element.22, f32[1024,64]{1,0:T(8,128)} %copy.47), kind=kLoop, calls=%fused_computation.7 | loop fusion | flops 33292288 | bytes 1376256 | tf_op jit(solution)/shard_map/reduce_min | solution.py:54
  409.4 1.3 copy.49
  410.7 2.7 minimum_minimum_fusion
  413.5 0.2 copy.56
  413.8 45.1 %add_reduce_fusion.2 = f32[1024,256]{1,0:T(8,128)S(1)} fusion(f32[64,256]{1,0:T(8,128)} %get-tuple-element.15, f32[1024,64]{1,0:T(8,128)S(1)} %copy.56), kind=kLoop, calls=%fused_computation.2 | loop fusion | flops 33292288 | bytes 1376256 | tf_op jit(solution)/shard_map/reduce_min | solution.py:54
  458.8 1.3 copy.58
  460.2 0.2 copy.61
  460.4 44.2 %add_reduce_fusion = f32[1024,256]{1,0:T(8,128)S(1)} fusion(f32[64,256]{1,0:T(8,128)S(1)} %copy-done.2, f32[1024,64]{1,0:T(8,128)S(1)} %copy.61), kind=kLoop, calls=%fused_computation | loop fusion | flops 33292288 | bytes 1376256 | tf_op jit(solution)/shard_map/reduce_min | solution.py:54
  504.6 1.3 copy.62
  505.9 0.2 copy.59
  506.1 44.2 %add_reduce_fusion.1 = f32[1024,256]{1,0:T(8,128)S(1)} fusion(f32[64,256]{1,0:T(8,128)S(1)} %copy-done.1, f32[1024,64]{1,0:T(8,128)S(1)} %copy.59), kind=kLoop, calls=%fused_computation.1 | loop fusion | flops 33292288 | bytes 1376256 | tf_op jit(solution)/shard_map/reduce_min | solution.py:54
  550.3 1.3 copy.60
  551.8 0.2 copy.55
  552.0 44.4 %add_reduce_fusion.3 = f32[1024,256]{1,0:T(8,128)S(1)} fusion(f32[64,256]{1,0:T(8,128)S(1)} %get-tuple-element.18, f32[1024,64]{1,0:T(8,128)S(1)} %copy.55), kind=kLoop, calls=%fused_computation.3 | loop fusion | flops 33292288 | bytes 1376256 | tf_op jit(solution)/shard_map/reduce_min | solution.py:54
  596.4 0.3 copy.57
  596.9 7.1 %fusion.10 = f32[1024,256]{0,1:T(8,128)S(1)} fusion(f32[1024,256]{1,0:T(8,128)S(1)} %bitcast.105, f32[1024,256]{0,1:T(8,128)} %copy.62, f32[1024,256]{0,1:T(8,128)} %copy.60, f32[1024,256]{0,1:T(8,128)S(1)} %copy.57, f32[1024,256]{0,1:T(8,128)} %copy.58, f32[256]{0:T(256)S(1)} %copy-done.24, f32[1024]{0:T(1024)S(1)} %copy-done.20, s32[1024]{0:T(1024)S(1)} %bitcast.123, ...), kind=kOutput, calls=%fused_computation.38 | convolution fusion | flops 818675712 | bytes 6615044 | tf_op jit(solution)/shard_map/if,jf->ij/dot_general | solution.py:38
  604.0 1.3 copy.63
  (131 shorter events, 1.9 us)
Async XLA Ops:
  6.5 43.9 %copy-start = (s32[32,10]{0,1:T(8,128)S(1)}, s32[32,10]{0,1:T(8,128)}, u32[]{:S(2)}) copy-start(s32[32,10]{0,1:T(8,128)} %param.4) | copy-start | bytes 3844
  8.4 41.2 %all-to-all-start.1 = ((f32[32,32,256]{2,1,0:T(8,128)}), f32[32,32,256]{2,1,0:T(8,128)S(1)}, u32[]{:S(2)}, u32[]{:S(2)}) async-start(f32[32,32,256]{2,1,0:T(8,128)} %broadcast_in_dim.5), calls=%async_computation.1 | async-start | bytes 2097152 | tf_op jit(solution)/shard_map/all_to_all | solution.py:15
  19.9 103.9 %all-gather.9.cloned.1.call-start = ((), (), s32[]{:S(2)}) async-start(), calls=%async_computation.3 | async-start | bytes 2359296 | tf_op jit(solution)/shard_map/all_gather | solution.py:32
  51.2 13.7 %all-to-all-start = ((s32[32,1,320]{2,1,0:T(1,128)}), s32[32,1,320]{2,1,0:T(1,128)S(1)}, u32[]{:S(2)}, u32[]{:S(2)}) async-start(s32[32,1,320]{2,1,0:T(1,128)} %reshape.106), calls=%async_computation | async-start | bytes 98304 | tf_op jit(solution)/shard_map/all_to_all | solution.py:15
  55.1 132.1 %all-gather.7.cloned.1.call-start = ((), (), s32[]{:S(2)}) async-start(), calls=%async_computation.2 | async-start | bytes 2359296 | tf_op jit(solution)/shard_map/all_gather | solution.py:32
  55.2 155.5 %copy-start.21 = (s32[1024]{0:T(1024)}, s32[1024]{0:T(1024)S(1)}, u32[]{:S(2)}) copy-start(s32[1024]{0:T(1024)S(1)} %iota_add_fusion) | copy-start | bytes 12292
  55.2 133.1 %copy-start.25 = (s32[256]{0:T(256)}, s32[256]{0:T(256)S(1)}, u32[]{:S(2)}) copy-start(s32[256]{0:T(256)S(1)} %get-tuple-element.88) | copy-start | bytes 3076
  123.3 65.0 %copy-start.27 = (s32[256,1]{0,1:T(1,128)}, s32[256,1]{0,1:T(1,128)S(1)}, u32[]{:S(2)}) copy-start(s32[256,1]{0,1:T(1,128)S(1)} %get-tuple-element.77) | copy-start | bytes 3076
  123.3 65.0 %copy-start.29 = (s32[256,1]{0,1:T(1,128)}, s32[256,1]{0,1:T(1,128)S(1)}, u32[]{:S(2)}) copy-start(s32[256,1]{0,1:T(1,128)S(1)} %get-tuple-element.78) | copy-start | bytes 3076
  123.3 65.0 %copy-start.31 = (s32[256,1]{0,1:T(1,128)}, s32[256,1]{0,1:T(1,128)S(1)}, u32[]{:S(2)}) copy-start(s32[256,1]{0,1:T(1,128)S(1)} %get-tuple-element.79) | copy-start | bytes 3076
  123.3 65.0 %copy-start.33 = (s32[256,1]{0,1:T(1,128)}, s32[256,1]{0,1:T(1,128)S(1)}, u32[]{:S(2)}) copy-start(s32[256,1]{0,1:T(1,128)S(1)} %get-tuple-element.80) | copy-start | bytes 3076
  123.3 65.0 %copy-start.35 = (s32[256,1]{0,1:T(1,128)}, s32[256,1]{0,1:T(1,128)S(1)}, u32[]{:S(2)}) copy-start(s32[256,1]{0,1:T(1,128)S(1)} %get-tuple-element.81) | copy-start | bytes 3076
  123.3 65.0 %copy-start.37 = (s32[256,1]{0,1:T(1,128)}, s32[256,1]{0,1:T(1,128)S(1)}, u32[]{:S(2)}) copy-start(s32[256,1]{0,1:T(1,128)S(1)} %get-tuple-element.82) | copy-start | bytes 3076
  123.3 65.0 %copy-start.39 = (s32[256,1]{0,1:T(1,128)}, s32[256,1]{0,1:T(1,128)S(1)}, u32[]{:S(2)}) copy-start(s32[256,1]{0,1:T(1,128)S(1)} %get-tuple-element.83) | copy-start | bytes 3076
  123.3 65.0 %copy-start.41 = (s32[256,1]{0,1:T(1,128)}, s32[256,1]{0,1:T(1,128)S(1)}, u32[]{:S(2)}) copy-start(s32[256,1]{0,1:T(1,128)S(1)} %get-tuple-element.84) | copy-start | bytes 3076
  123.3 65.0 %copy-start.43 = (s32[256,1]{0,1:T(1,128)}, s32[256,1]{0,1:T(1,128)S(1)}, u32[]{:S(2)}) copy-start(s32[256,1]{0,1:T(1,128)S(1)} %get-tuple-element.85) | copy-start | bytes 3076
  123.4 65.0 %copy-start.45 = (s32[256,1]{0,1:T(1,128)}, s32[256,1]{0,1:T(1,128)S(1)}, u32[]{:S(2)}) copy-start(s32[256,1]{0,1:T(1,128)S(1)} %get-tuple-element.86) | copy-start | bytes 3076
  123.4 87.4 %copy-start.3 = (s32[1024,1]{0,1:T(1,128)}, s32[1024,1]{0,1:T(1,128)S(1)}, u32[]{:S(2)}) copy-start(s32[1024,1]{0,1:T(1,128)S(1)} %get-tuple-element.57) | copy-start | bytes 12292
  123.4 87.3 %copy-start.5 = (s32[1024,1]{0,1:T(1,128)}, s32[1024,1]{0,1:T(1,128)S(1)}, u32[]{:S(2)}) copy-start(s32[1024,1]{0,1:T(1,128)S(1)} %get-tuple-element.58) | copy-start | bytes 12292
  123.4 87.3 %copy-start.7 = (s32[1024,1]{0,1:T(1,128)}, s32[1024,1]{0,1:T(1,128)S(1)}, u32[]{:S(2)}) copy-start(s32[1024,1]{0,1:T(1,128)S(1)} %get-tuple-element.59) | copy-start | bytes 12292
  123.4 87.3 %copy-start.9 = (s32[1024,1]{0,1:T(1,128)}, s32[1024,1]{0,1:T(1,128)S(1)}, u32[]{:S(2)}) copy-start(s32[1024,1]{0,1:T(1,128)S(1)} %get-tuple-element.60) | copy-start | bytes 12292
  123.4 87.3 %copy-start.11 = (s32[1024,1]{0,1:T(1,128)}, s32[1024,1]{0,1:T(1,128)S(1)}, u32[]{:S(2)}) copy-start(s32[1024,1]{0,1:T(1,128)S(1)} %get-tuple-element.61) | copy-start | bytes 12292
  123.5 87.3 %copy-start.13 = (s32[1024,1]{0,1:T(1,128)}, s32[1024,1]{0,1:T(1,128)S(1)}, u32[]{:S(2)}) copy-start(s32[1024,1]{0,1:T(1,128)S(1)} %get-tuple-element.62) | copy-start | bytes 12292
  123.5 87.3 %copy-start.15 = (s32[1024,1]{0,1:T(1,128)}, s32[1024,1]{0,1:T(1,128)S(1)}, u32[]{:S(2)}) copy-start(s32[1024,1]{0,1:T(1,128)S(1)} %get-tuple-element.63) | copy-start | bytes 12292
  123.5 87.3 %copy-start.17 = (s32[1024,1]{0,1:T(1,128)}, s32[1024,1]{0,1:T(1,128)S(1)}, u32[]{:S(2)}) copy-start(s32[1024,1]{0,1:T(1,128)S(1)} %get-tuple-element.64) | copy-start | bytes 12292
  123.8 87.1 %copy-start.19 = (f32[1024]{0:T(1024)}, f32[1024]{0:T(1024)S(1)}, u32[]{:S(2)}) copy-start(f32[1024]{0:T(1024)S(1)} %add.417) | copy-start | bytes 12292
  188.3 7.3 %copy-start.23 = (f32[256]{0:T(256)}, f32[256]{0:T(256)S(1)}, u32[]{:S(2)}) copy-start(f32[256]{0:T(256)S(1)} %fusion.25) | copy-start | bytes 3076
  413.7 46.6 %copy-start.2 = (f32[64,256]{1,0:T(8,128)S(1)}, f32[64,256]{1,0:T(8,128)}, u32[]{:S(2)}) copy-start(f32[64,256]{1,0:T(8,128)} %get-tuple-element.16) | copy-start | bytes 196612
  460.4 45.7 %copy-start.1 = (f32[64,256]{1,0:T(8,128)S(1)}, f32[64,256]{1,0:T(8,128)}, u32[]{:S(2)}) copy-start(f32[64,256]{1,0:T(8,128)} %get-tuple-element.17) | copy-start | bytes 196612
  551.6 45.1 %copy-start.4 = (s32[1024,1]{0,1:T(1,128)S(1)}, s32[1024,1]{0,1:T(1,128)}, u32[]{:S(2)}) copy-start(s32[1024,1]{0,1:T(1,128)} %copy-done.3) | copy-start | bytes 12292
  551.6 45.1 %copy-start.6 = (s32[1024,1]{0,1:T(1,128)S(1)}, s32[1024,1]{0,1:T(1,128)}, u32[]{:S(2)}) copy-start(s32[1024,1]{0,1:T(1,128)} %copy-done.5) | copy-start | bytes 12292
  551.6 45.1 %copy-start.8 = (s32[1024,1]{0,1:T(1,128)S(1)}, s32[1024,1]{0,1:T(1,128)}, u32[]{:S(2)}) copy-start(s32[1024,1]{0,1:T(1,128)} %copy-done.7) | copy-start | bytes 12292
  551.6 45.1 %copy-start.10 = (s32[1024,1]{0,1:T(1,128)S(1)}, s32[1024,1]{0,1:T(1,128)}, u32[]{:S(2)}) copy-start(s32[1024,1]{0,1:T(1,128)} %copy-done.9) | copy-start | bytes 12292
  551.6 45.1 %copy-start.12 = (s32[1024,1]{0,1:T(1,128)S(1)}, s32[1024,1]{0,1:T(1,128)}, u32[]{:S(2)}) copy-start(s32[1024,1]{0,1:T(1,128)} %copy-done.11) | copy-start | bytes 12292
  551.6 45.1 %copy-start.14 = (s32[1024,1]{0,1:T(1,128)S(1)}, s32[1024,1]{0,1:T(1,128)}, u32[]{:S(2)}) copy-start(s32[1024,1]{0,1:T(1,128)} %copy-done.13) | copy-start | bytes 12292
  551.7 45.1 %copy-start.16 = (s32[1024,1]{0,1:T(1,128)S(1)}, s32[1024,1]{0,1:T(1,128)}, u32[]{:S(2)}) copy-start(s32[1024,1]{0,1:T(1,128)} %copy-done.15) | copy-start | bytes 12292
  551.7 45.1 %copy-start.18 = (s32[1024,1]{0,1:T(1,128)S(1)}, s32[1024,1]{0,1:T(1,128)}, u32[]{:S(2)}) copy-start(s32[1024,1]{0,1:T(1,128)} %copy-done.17) | copy-start | bytes 12292
  551.7 45.1 %copy-start.20 = (f32[1024]{0:T(1024)S(1)}, f32[1024]{0:T(1024)}, u32[]{:S(2)}) copy-start(f32[1024]{0:T(1024)} %copy-done.19) | copy-start | bytes 12292
  551.7 45.1 %copy-start.22 = (s32[1024]{0:T(1024)S(1)}, s32[1024]{0:T(1024)}, u32[]{:S(2)}) copy-start(s32[1024]{0:T(1024)} %copy-done.21) | copy-start | bytes 12292
  551.7 45.1 %copy-start.24 = (f32[256]{0:T(256)S(1)}, f32[256]{0:T(256)}, u32[]{:S(2)}) copy-start(f32[256]{0:T(256)} %copy-done.23) | copy-start | bytes 3076
  551.7 45.1 %copy-start.26 = (s32[256]{0:T(256)S(1)}, s32[256]{0:T(256)}, u32[]{:S(2)}) copy-start(s32[256]{0:T(256)} %copy-done.25) | copy-start | bytes 3076
  551.7 45.1 %copy-start.28 = (s32[256,1]{0,1:T(1,128)S(1)}, s32[256,1]{0,1:T(1,128)}, u32[]{:S(2)}) copy-start(s32[256,1]{0,1:T(1,128)} %copy-done.27) | copy-start | bytes 3076
  551.7 45.1 %copy-start.30 = (s32[256,1]{0,1:T(1,128)S(1)}, s32[256,1]{0,1:T(1,128)}, u32[]{:S(2)}) copy-start(s32[256,1]{0,1:T(1,128)} %copy-done.29) | copy-start | bytes 3076
  551.7 45.1 %copy-start.32 = (s32[256,1]{0,1:T(1,128)S(1)}, s32[256,1]{0,1:T(1,128)}, u32[]{:S(2)}) copy-start(s32[256,1]{0,1:T(1,128)} %copy-done.31) | copy-start | bytes 3076
  551.7 45.1 %copy-start.34 = (s32[256,1]{0,1:T(1,128)S(1)}, s32[256,1]{0,1:T(1,128)}, u32[]{:S(2)}) copy-start(s32[256,1]{0,1:T(1,128)} %copy-done.33) | copy-start | bytes 3076
  551.8 45.1 %copy-start.36 = (s32[256,1]{0,1:T(1,128)S(1)}, s32[256,1]{0,1:T(1,128)}, u32[]{:S(2)}) copy-start(s32[256,1]{0,1:T(1,128)} %copy-done.35) | copy-start | bytes 3076
  551.8 45.1 %copy-start.38 = (s32[256,1]{0,1:T(1,128)S(1)}, s32[256,1]{0,1:T(1,128)}, u32[]{:S(2)}) copy-start(s32[256,1]{0,1:T(1,128)} %copy-done.37) | copy-start | bytes 3076
  551.8 45.1 %copy-start.40 = (s32[256,1]{0,1:T(1,128)S(1)}, s32[256,1]{0,1:T(1,128)}, u32[]{:S(2)}) copy-start(s32[256,1]{0,1:T(1,128)} %copy-done.39) | copy-start | bytes 3076
  551.8 45.1 %copy-start.42 = (s32[256,1]{0,1:T(1,128)S(1)}, s32[256,1]{0,1:T(1,128)}, u32[]{:S(2)}) copy-start(s32[256,1]{0,1:T(1,128)} %copy-done.41) | copy-start | bytes 3076
  551.8 45.1 %copy-start.44 = (s32[256,1]{0,1:T(1,128)S(1)}, s32[256,1]{0,1:T(1,128)}, u32[]{:S(2)}) copy-start(s32[256,1]{0,1:T(1,128)} %copy-done.43) | copy-start | bytes 3076
  551.8 45.1 %copy-start.46 = (s32[256,1]{0,1:T(1,128)S(1)}, s32[256,1]{0,1:T(1,128)}, u32[]{:S(2)}) copy-start(s32[256,1]{0,1:T(1,128)} %copy-done.45) | copy-start | bytes 3076
Sparse Core Ops, SparseCore 0:
  50.6 37.8 all-gather.8
  123.9 36.2 all-gather.6
where the time goes:
time: 616 us; the launch traced here: 612 us
  other arithmetic  444 us (72%)
  blocking collectives  56.4 us (9%)
  waiting for transfers between devices  38.8 us (6%)
  local copies, waits for them, and re-layouts  25.2 us (4%)
  matrix products  17 us (3%)
  between operations  15.5 us (3%)
  starting transfers between devices  15.4 us (2%)
    reduce_min x24, other arithmetic, min_plus(): jnp.min(left[:, start:start + step, None] + right[None, start:start + ste...  438 us
    all_gather x2, blocking collectives, picked(): lax.all_gather(value, axis)  56.4 us
    all_to_all x2, waiting for transfers between devices, copy_for_each(): lax.all_to_all(jnp.broadcast_to(value[None], (size, *value.shape)), axis,...  38.7 us
    dot_general x4, matrix products, weights_of(): jnp.einsum('if,jf->ij', points_a, points_b, precision=lax.Precision.HIGHEST)  17 us
    all_to_all x2, starting transfers between devices, copy_for_each(): lax.all_to_all(jnp.broadcast_to(value[None], (size, *value.shape)), axis,...  15.3 us
  transfers between devices with their start and end apart: 4, of which 2 were waited for; matrix products, arithmetic and copies ran while one was open for 11% of the time, Pallas kernels for 0%

commit v1 on v0

v1 whole, which is shorter than its diff:
```python
import functools

import jax
import jax.numpy as jnp
from jax import lax
from jax.experimental import pallas as pl
from jax.experimental.pallas import tpu as pltpu
from jax.sharding import PartitionSpec as P

PB = 256
SQUARINGS = 3
K = 10
far_weight = 3.0
LANES = 128


def copy_for_each(value, axis):
    size = lax.axis_size(axis)
    return lax.all_to_all(
        jnp.broadcast_to(value[None], (size, *value.shape)), axis, 0, 0, tiled=True
    )


def joined_along(pieces, dim):
    dims = list(pieces.shape[1:])
    dims[dim] *= pieces.shape[0]
    return jnp.moveaxis(pieces, 0, dim).reshape(dims)


def collect(value, axis, dim):
    pieces = copy_for_each(value, axis)
    return joined_along(pieces, dim)


def picked(value, axis, root):
    return lax.dynamic_index_in_dim(lax.all_gather(value, axis), root, 0, keepdims=False)


def dot_nt(a, b):
    return lax.dot_general(
        a, b, (((1,), (1,)), ((), ())),
        precision=lax.Precision.HIGHEST, preferred_element_type=jnp.float32,
    )


def lane_norms(points):
    ones = jnp.ones((8, points.shape[1]), jnp.float32)
    return dot_nt(ones, points * points)[:1]


def weigh(pts_a, lists_a, base_a, pts_b, lists_bt, norm_b, base_b, out, step=32):
    width = pts_b.shape[0]

    def chunk(t, carry):
        rows = pl.ds(pl.multiple_of(t * step, step), step)
        a = pts_a[rows, :]
        norm_a = jnp.sum(a * a, axis=1, keepdims=True)
        inner = dot_nt(a, pts_b[...])
        squares = norm_a + norm_b[...] - 2.0 * inner
        length = jnp.sqrt(jnp.maximum(squares, 0.0))
        ids_a = base_a + t * step + lax.broadcasted_iota(jnp.int32, (step, width), 0)
        ids_b = base_b + lax.broadcasted_iota(jnp.int32, (step, width), 1)
        la = lists_a[rows, :]
        linked = ids_a == ids_b
        for slot in range(K):
            linked = linked | (la[:, slot : slot + 1] == ids_b)
            linked = linked | (lists_bt[slot : slot + 1, :] == ids_a)
        weighted = jnp.where(linked, length, far_weight * length)
        weighted = jnp.where(ids_a == ids_b, 0.0, weighted)
        for tile in range(width // LANES):
            out[tile, rows, :] = weighted[:, tile * LANES : (tile + 1) * LANES]
        return carry

    lax.fori_loop(0, pts_a.shape[0] // step, chunk, 0)


def min_plus(left, right, init, out, rows, first, count, tiles):
    halves = left.shape[0]
    split = (rows // 8, 8, LANES)

    def block(t, carry):
        at = pl.ds(pl.multiple_of((first + t) * rows, rows), rows)

        def half(h, best):
            piece = left[h, at, :].reshape(split)
            best = list(best)
            base = h * LANES
            for k in range(LANES):
                down = jnp.broadcast_to(piece[:, :, k : k + 1], split)
                for n, tile in enumerate(tiles):
                    row = right[tile, pl.ds(base + k, 8, stride=0), :]
                    best[n] = jnp.minimum(best[n], down + row[None])
            return tuple(best)

        best = tuple(init[tile, at, :].reshape(split) for tile in tiles)
        best = lax.fori_loop(0, halves, half, best)
        for n, tile in enumerate(tiles):
            out[tile, at, :] = best[n].reshape(rows, LANES)
        return carry

    lax.fori_loop(0, count, block, 0)


def body(base, rp, rlt, cp, cl, clt, pp, plists, plt_, o_ref, ct, bt, ka, kb, xt, wt, nr, npv, nc):
    row_base, col_base, pivot_base = base[0], base[1], base[2]
    npv[...] = lane_norms(pp[...])
    nr[...] = lane_norms(rp[...])
    weigh(pp, plists, pivot_base, pp, plt_, npv, pivot_base, ka)
    for turn in range(SQUARINGS + 1):
        src, dst = (ka, kb) if turn % 2 == 0 else (kb, ka)
        min_plus(src, src, src, dst, 128, 0, 1, (0, 1))
        min_plus(src, src, src, dst, 128, 1, 1, (1,))
        dst[0, 128:256, :] = dst[1, 0:128, :].T
    closed = ka if (SQUARINGS + 1) % 2 == 0 else kb
    weigh(cp, cl, col_base, pp, plt_, npv, pivot_base, bt)
    min_plus(bt, closed, bt, xt, 128, 0, 2, (0, 1))
    weigh(pp, plists, pivot_base, rp, rlt, nr, row_base, ct)
    weigh(cp, cl, col_base, rp, rlt, nr, row_base, wt)
    min_plus(xt, ct, wt, wt, 32, 0, 8, tuple(range(8)))
    for t in range(8):
        o_ref[t * LANES : (t + 1) * LANES, :] = wt[t].T


def tile_of(base, rp, rl, cp, cl, pp, plists):
    rows, cols = rp.shape[0], cp.shape[0]

    def across(lists):
        return jnp.pad(lists.T, ((0, 16 - K), (0, 0)))

    def down(lists):
        return jnp.pad(lists, ((0, 0), (0, LANES - K)))

    vmem = pl.BlockSpec(memory_space=pltpu.VMEM)
    f32 = jnp.float32
    return pl.pallas_call(
        body,
        out_shape=jax.ShapeDtypeStruct((rows, cols), f32),
        in_specs=[pl.BlockSpec(memory_space=pltpu.SMEM)] + [vmem] * 8,
        out_specs=vmem,
        scratch_shapes=[
            pltpu.VMEM((rows // LANES, PB, LANES), f32),
            pltpu.VMEM((PB // LANES, cols, LANES), f32),
            pltpu.VMEM((PB // LANES, PB, LANES), f32),
            pltpu.VMEM((PB // LANES, PB, LANES), f32),
            pltpu.VMEM((PB // LANES, cols, LANES), f32),
            pltpu.VMEM((rows // LANES, cols, LANES), f32),
            pltpu.VMEM((1, rows), f32),
            pltpu.VMEM((1, PB), f32),
            pltpu.VMEM((1, cols), f32),
        ],
        compiler_params=pltpu.CompilerParams(vmem_limit_bytes=40 << 20),
    )(base, rp, across(rl), cp, down(cl), across(cl), pp, down(plists), across(plists))


def local(features, neighbors, pivot):
    row_points, row_lists = (collect(features, "col", 0), collect(neighbors, "col", 0))
    row_count = row_points.shape[0]
    col_count = row_count * lax.axis_size("row") // lax.axis_size("col")
    row_index = lax.axis_index("row")
    col_index = lax.axis_index("col")
    offset = jnp.clip(col_index * col_count - row_index * row_count, 0, row_count - col_count)
    col_points = lax.dynamic_slice_in_dim(row_points, offset, col_count, 0)
    col_lists = lax.dynamic_slice_in_dim(row_lists, offset, col_count, 0)
    owner_row = col_index * col_count // row_count
    col_points, col_lists = (
        picked(col_points, "row", owner_row),
        picked(col_lists, "row", owner_row),
    )
    pivot_base = pivot[0] * PB
    pivot_row = pivot_base // row_count
    row_offset = jnp.clip(pivot_base - row_index * row_count, 0, row_count - PB)
    pivot_feats = lax.dynamic_slice_in_dim(row_points, row_offset, PB, 0)
    pivot_lists = lax.dynamic_slice_in_dim(row_lists, row_offset, PB, 0)
    pivot_feats, pivot_lists = (
        picked(pivot_feats, "row", pivot_row),
        picked(pivot_lists, "row", pivot_row),
    )
    base = jnp.stack([row_index * row_count, col_index * col_count, pivot_base]).astype(jnp.int32)
    return tile_of(base, row_points, row_lists, col_points, col_lists, pivot_feats, pivot_lists)


def solution(mesh):
    return jax.shard_map(
        local,
        mesh=mesh,
        in_specs=(P(("row", "col"), None), P(("row", "col"), None), P()),
        out_specs=P("row", "col"),
        check_vma=False,
    )
```

time: 616 us -> 249 us (0.40)
  the two profiles are of different devices: /device:TPU:6 before, /device:TPU:1 now
where the time goes in v1:
time: 249 us; the launch traced here: 245 us
  Pallas kernels  106 us (43%)
  waiting for transfers between devices  51.7 us (21%)
  blocking collectives  47.6 us (19%)
  starting transfers between devices  17.6 us (7%)
  between operations  14.3 us (6%)
  local copies, waits for them, and re-layouts  6.74 us (3%)
    pallas_call x1, Pallas kernels, tile_of(): pl.pallas_call(body, out_shape=jax.ShapeDtypeStruct((rows, cols), f32), i...  106 us
    all_gather x2, blocking collectives, picked(): lax.all_gather(value, axis)  47.6 us
    all_to_all x2, waiting for transfers between devices, copy_for_each(): lax.all_to_all(jnp.broadcast_to(value[None], (size, *value.shape)), axis,...  37.6 us
    all_to_all x2, starting transfers between devices, copy_for_each(): lax.all_to_all(jnp.broadcast_to(value[None], (size, *value.shape)), axis,...  17.6 us
    all_gather x2, waiting for transfers between devices, picked(): lax.all_gather(value, axis)  13.4 us
  transfers between devices with their start and end apart: 4, of which 3 were waited for; matrix products, arithmetic and copies ran while one was open for 2% of the time, Pallas kernels for 0%

profile of v1, /device:TPU:1, one launch (start us, length us, event | category | flops | bytes accessed | tf_op | source)
XLA Modules:
  0.0 244.5 jit_solution(10717937342231205789)
XLA Ops:
  6.5 0.0 copy-start
  6.5 1.9 broadcast_in_dim.4
  8.4 12.7 %all-to-all-start = ((f32[32,32,256]{2,1,0:T(8,128)}), f32[32,32,256]{2,1,0:T(8,128)S(1)}, u32[]{:S(2)}, u32[]{:S(2)}) async-start(f32[32,32,256]{2,1,0:T(8,128)} %broadcast_in_dim.4), calls=%async_computation | async-start | bytes 2097152 | tf_op jit(solution)/shard_map/all_to_all | solution.py:19
  21.1 0.0 all-gather.7.cloned.1.call-start
  21.9 27.9 %all-to-all-done = f32[32,32,256]{2,1,0:T(8,128)S(1)} async-done(((f32[32,32,256]{2,1,0:T(8,128)}), f32[32,32,256]{2,1,0:T(8,128)S(1)}, u32[]{:S(2)}, u32[]{:S(2)}) %all-to-all-start) | async-done | bytes 1048608 | tf_op jit(solution)/shard_map/all_to_all | solution.py:19
  49.8 0.8 constant_dynamic-slice_fusion.2
  50.6 0.0 all-gather.7.cloned.1.call-update
  50.6 0.0 all-gather.9.cloned.1.call-start
  50.7 0.7 all-gather.9.cloned.1.call-update
  51.4 0.0 copy-done
  51.4 0.8 reshape.17
  52.2 4.8 %all-to-all-start.1 = ((s32[32,1,320]{2,1,0:T(1,128)}), s32[32,1,320]{2,1,0:T(1,128)S(1)}, u32[]{:S(2)}, u32[]{:S(2)}) async-start(s32[32,1,320]{2,1,0:T(1,128)} %reshape.17), calls=%async_computation.1 | async-start | bytes 98304 | tf_op jit(solution)/shard_map/all_to_all | solution.py:19
  57.0 0.1 pad_add_fusion.base
  57.1 9.7 %all-to-all-done.1 = s32[32,1,320]{2,1,0:T(1,128)S(1)} async-done(((s32[32,1,320]{2,1,0:T(1,128)}), s32[32,1,320]{2,1,0:T(1,128)S(1)}, u32[]{:S(2)}, u32[]{:S(2)}) %all-to-all-start.1) | async-done | bytes 40992 | tf_op jit(solution)/shard_map/all_to_all | solution.py:19
  66.8 0.6 broadcast.14
  67.4 0.7 reduce
  68.1 0.1 reshape.18
  68.2 0.1 copy.8
  68.3 0.1 reshape.12
  68.4 0.1 constant_dynamic-slice_fusion.1
  68.5 23.8 %all-gather.1 = s32[2048,10]{0,1:T(8,128)S(1)} all-gather(s32[256,10]{0,1:T(8,128)S(1)} %get-tuple-element.8), channel_id=3, replica_groups=mesh['row'=8,'col'=32] {'row'}, dimensions={0}, use_global_device_ids=true | all-gather | bytes 92160 | tf_op jit(solution)/shard_map/all_gather | solution.py:36
  92.3 0.1 copy.17
  92.5 23.8 %all-gather.3 = s32[2048,10]{0,1:T(8,128)S(1)} all-gather(s32[256,10]{0,1:T(8,128)S(1)} %get-tuple-element.7), channel_id=5, replica_groups=mesh['row'=8,'col'=32] {'row'}, dimensions={0}, use_global_device_ids=true | all-gather | bytes 92160 | tf_op jit(solution)/shard_map/all_gather | solution.py:36
  116.3 0.1 copy.18
  116.5 0.0 all-gather.7.cloned.1.call-done
  116.6 1.0 dynamic-slice_bitcast_fusion.1.cp
  117.5 13.4 %all-gather.9.cloned.1.call-done = f32[2048,256]{1,0:T(8,128)} async-done(((f32[256,256]{1,0:T(8,128)}), f32[2048,256]{1,0:T(8,128)}) %all-gather.9.cloned.1.call-update) | async-done | bytes 2097168 | tf_op jit(solution)/shard_map/all_gather | solution.py:36
  130.9 1.0 dynamic-slice_bitcast_fusion.pp
  131.9 105.8 %shard_map.37 = f32[1024,256]{1,0:T(8,128)} custom-call(s32[3]{0:T(128)S(1)} %pad_add_fusion.base, f32[1024,256]{1,0:T(8,128)S(1)} %bitcast.41, s32[16,1024]{1,0:T(8,128)S(1)} %pad.18.rlt, f32[256,256]{1,0:T(8,128)S(1)} %dynamic-slice_bitcast_fusion.1.cp, s32[256,128]{1,0:T(8,128)S(1)} %pad.19.clone.cl, s32[16,256]{1,0:T(8,128)S(1)} %pad.20.clt, ...), custom_call_target="tpu_custom_call" | custom-call | tf_op jit(solution)/shard_map/pallas_call | solution.py:135
  (14 shorter events, 0.2 us)
Async XLA Ops:
  6.5 44.8 %copy-start = (s32[32,10]{0,1:T(8,128)S(1)}, s32[32,10]{0,1:T(8,128)}, u32[]{:S(2)}) copy-start(s32[32,10]{0,1:T(8,128)} %param.4) | copy-start | bytes 3844
  8.4 41.4 %all-to-all-start = ((f32[32,32,256]{2,1,0:T(8,128)}), f32[32,32,256]{2,1,0:T(8,128)S(1)}, u32[]{:S(2)}, u32[]{:S(2)}) async-start(f32[32,32,256]{2,1,0:T(8,128)} %broadcast_in_dim.4), calls=%async_computation | async-start | bytes 2097152 | tf_op jit(solution)/shard_map/all_to_all | solution.py:19
  21.1 95.4 %all-gather.7.cloned.1.call-start = ((), (), s32[]{:S(2)}) async-start(), calls=%async_computation.2 | async-start | bytes 2359296 | tf_op jit(solution)/shard_map/all_gather | solution.py:36
  50.6 80.3 %all-gather.9.cloned.1.call-start = ((), (), s32[]{:S(2)}) async-start(), calls=%async_computation.3 | async-start | bytes 2359296 | tf_op jit(solution)/shard_map/all_gather | solution.py:36
  52.2 14.6 %all-to-all-start.1 = ((s32[32,1,320]{2,1,0:T(1,128)}), s32[32,1,320]{2,1,0:T(1,128)S(1)}, u32[]{:S(2)}, u32[]{:S(2)}) async-start(s32[32,1,320]{2,1,0:T(1,128)} %reshape.17), calls=%async_computation.1 | async-start | bytes 98304 | tf_op jit(solution)/shard_map/all_to_all | solution.py:19
Sparse Core Ops, SparseCore 0:
  50.7 35.6 all-gather.6
  88.2 42.6 all-gather.8

commit v2 on v1

v2 whole, which is shorter than its diff:
```python
import functools

import jax
import jax.numpy as jnp
from jax import lax
from jax.experimental import pallas as pl
from jax.experimental.pallas import tpu as pltpu
from jax.sharding import PartitionSpec as P

PB = 256
SQUARINGS = 3
K = 10
far_weight = 3.0
LANES = 128


def copy_for_each(value, axis):
    size = lax.axis_size(axis)
    return lax.all_to_all(
        jnp.broadcast_to(value[None], (size, *value.shape)), axis, 0, 0, tiled=True
    )


def joined_along(pieces, dim):
    dims = list(pieces.shape[1:])
    dims[dim] *= pieces.shape[0]
    return jnp.moveaxis(pieces, 0, dim).reshape(dims)


def collect(value, axis, dim):
    pieces = copy_for_each(value, axis)
    return joined_along(pieces, dim)


def picked(value, axis, root):
    return lax.dynamic_index_in_dim(lax.all_gather(value, axis), root, 0, keepdims=False)


def dot(a, b, dims):
    return lax.dot_general(
        a, b, (dims, ((), ())),
        precision=lax.Precision.HIGHEST, preferred_element_type=jnp.float32,
    )


def norms_down(points, out):
    p = points[...]
    out[...] = dot(p * p, jnp.ones((p.shape[1], LANES), jnp.float32), ((1,), (0,)))


def norms_across(points, out):
    def chunk(t, carry):
        p = points[pl.ds(pl.multiple_of(t * LANES, LANES), LANES), :]
        out[t] = dot(jnp.ones((8, p.shape[1]), jnp.float32), p * p, ((1,), (1,)))
        return carry

    lax.fori_loop(0, points.shape[0] // LANES, chunk, 0)


def bits_of(lists, base, words):
    n = lists.shape[1]
    word = lax.broadcasted_iota(jnp.int32, (words, n), 0)
    found = jnp.zeros((words, n), jnp.int32)
    for slot in range(K):
        at = lists[slot : slot + 1, :] - base
        bit = jnp.left_shift(jnp.int32(1), at & 31)
        found = found | jnp.where(jnp.right_shift(at, 5) == word, bit, 0)
    return found


def weigh(pts_a, lists_a, base_a, norm_a, pts_b, lists_b, base_b, norm_b, out, wa, wb):
    count, width = pts_a.shape[0], pts_b.shape[0]
    tiles = width // LANES

    bits = bits_of(lists_a, base_b, width // 32)
    pad = jnp.zeros((LANES - width // 32, count), jnp.int32)
    wa[...] = jnp.concatenate([bits, pad], axis=0).T
    bits = bits_of(lists_b, base_a, count // 32)
    for tile in range(tiles):
        wb[tile] = bits[:, tile * LANES : (tile + 1) * LANES]

    a = pts_a[...]

    def products(t, carry):
        b = pts_b[pl.ds(pl.multiple_of(t * 256, 256), 256), :]
        inner = dot(a, b, ((1,), (1,)))
        out[2 * t] = inner[:, :LANES]
        out[2 * t + 1] = inner[:, LANES:]
        return carry

    lax.fori_loop(0, width // 256, products, 0)

    lane = lax.broadcasted_iota(jnp.int32, (32, LANES), 1)
    down = lax.broadcasted_iota(jnp.int32, (32, LANES), 0)

    def group(n, carry):
        t, g = n // (count // 32), n % (count // 32)
        rows = pl.ds(pl.multiple_of(g * 32, 32), 32)
        squares = norm_a[rows, :] + jnp.tile(norm_b[t], (4, 1)) - 2.0 * out[t, rows, :]
        squares = jnp.maximum(squares, 0.0)
        length = squares * lax.rsqrt(jnp.maximum(squares, 1.2e-38))
        listed = lanes_of(wa[rows, :], lane // 32 + 4 * t)
        listed = jnp.right_shift(listed, lane & 31)
        lists = jnp.tile(wb[t, pl.ds(g, 8, stride=0), :], (4, 1))
        listed = listed | jnp.right_shift(lists, down)
        weighted = jnp.where((listed & 1) == 1, length, far_weight * length)
        same = (down - lane) == (base_b - base_a + t * LANES - g * 32)
        out[t, rows, :] = jnp.where(same, 0.0, weighted)
        return carry

    lax.fori_loop(0, tiles * (count // 32), group, 0)


AHEAD = 6


def lanes_of(piece, index):
    dims = lax.GatherDimensionNumbers(
        offset_dims=(), collapsed_slice_dims=(1,), start_index_map=(1,),
        operand_batching_dims=(0,), start_indices_batching_dims=(0,),
    )
    return lax.gather(
        piece, index[:, :, None], dims, (1, 1), mode=lax.GatherScatterMode.PROMISE_IN_BOUNDS
    )


def min_plus(left, right, fold, done, unroll=32, rows=16, together=1):
    tiles, depth = right.shape[0], right.shape[1]
    halves = left.shape[0]
    depth = depth // halves
    subs = rows // 8
    pattern = lax.broadcasted_iota(jnp.int32, (8, LANES), 1) // (LANES // fold)

    def block(t, carry):
        at = pl.ds(pl.multiple_of(t * rows, rows), rows)
        best = tuple(jnp.full((8, LANES), jnp.inf, jnp.float32) for _ in range(tiles * subs))

        for h in range(halves):
            pieces = [
                left[h, pl.ds(pl.multiple_of(t * rows + 8 * s, 8), 8), :] for s in range(subs)
            ]

            def spread_of(at, u):
                index = (at + u * fold) & (LANES - 1)
                return tuple(lanes_of(piece, index) for piece in pieces)

            def some(c, carry):
                ahead, best = list(carry[0]), list(carry[1])
                first = pattern + c * (unroll * fold)
                for u in range(unroll):
                    ahead.append(spread_of(first, u + AHEAD))
                    downs = ahead.pop(0)
                    for tile in range(tiles):
                        row = right[tile, pl.ds(h * depth + c * unroll + u, 8, stride=0), :]
                        for s, down in enumerate(downs):
                            n = tile * subs + s
                            best[n] = jnp.minimum(best[n], down + row)
                return tuple(ahead), tuple(best)

            ahead = tuple(spread_of(pattern, u) for u in range(AHEAD))
            _, best = lax.fori_loop(0, depth // unroll, some, (ahead, best))
        done(at, [jnp.concatenate(best[n * subs : n * subs + subs], axis=0) for n in range(tiles)])
        return carry

    def blocks(t, carry):
        for n in range(together):
            block(t * together + n, carry)
        return carry

    lax.fori_loop(0, left.shape[1] // rows // together, blocks, 0)


FOLD = 4


def folded(wide, right):
    lane = lax.broadcasted_iota(jnp.int32, (PB // FOLD, LANES), 1) // (LANES // FOLD)
    for tile in range(wide.shape[0]):
        piece = wide[tile, pl.ds(0, PB // FOLD, stride=FOLD), :]
        for c in range(1, FOLD):
            other = wide[tile, pl.ds(c, PB // FOLD, stride=FOLD), :]
            piece = jnp.where(lane == c, other, piece)
        right[tile] = piece


def gathered(parts):
    group = lax.broadcasted_iota(jnp.int32, parts[0].shape, 1) // (LANES // FOLD)
    tile = parts[0]
    for c in range(1, FOLD):
        tile = jnp.where(group == c, parts[c], tile)
    return tile


def reduced(piece):
    piece = jnp.minimum(piece, pltpu.roll(piece, 64, 1))
    return jnp.minimum(piece, pltpu.roll(piece, 32, 1))


def spread(tiles, wide):
    lane = lax.broadcasted_iota(jnp.int32, (32, LANES), 1) % (LANES // FOLD)
    for g in range(wide.shape[0]):

        def chunk(t, carry):
            rows = pl.ds(pl.multiple_of(t * 32, 32), 32)
            piece = tiles[g // FOLD, rows, :]
            wide[g, rows, :] = lanes_of(piece, lane + 32 * (g % FOLD))
            return carry

        lax.fori_loop(0, PB // 32, chunk, 0)


def body(base, rp, rlt, cp, clt, pp, plt_, o_ref, ct, bt, ka, wide, fold, xt, wt,
         nra, npd, npa, ncd, wa, wb):
    row_base, col_base, pivot_base = base[0], base[1], base[2]
    norms_across(rp, nra)
    norms_across(pp, npa)
    norms_down(pp, npd)
    norms_down(cp, ncd)
    weigh(pp, plt_, pivot_base, npd, pp, plt_, pivot_base, npa, ka, wa, wb)
    spread(ka, wide)

    def square(turn, carry):
        folded(wide, fold)

        def done(at, best):
            best = [reduced(b) for b in best]
            for g in range(8):
                wide[g, at, :] = best[g]
            for tile in range(2):
                kept = gathered(best[FOLD * tile : FOLD * tile + FOLD])
                ka[tile, at, :] = jnp.minimum(ka[tile, at, :], kept)

        min_plus(ka, fold, FOLD, done)
        return carry

    lax.fori_loop(0, SQUARINGS + 1, square, 0)
    folded(wide, fold)
    weigh(cp, clt, col_base, ncd, pp, plt_, pivot_base, npa, bt, wa, wb)

    def done(at, best):
        best = [reduced(b) for b in best]
        for tile in range(2):
            kept = gathered(best[FOLD * tile : FOLD * tile + FOLD])
            xt[tile, at, :] = jnp.minimum(bt[tile, at, :], kept)

    min_plus(bt, fold, FOLD, done)
    weigh(pp, plt_, pivot_base, npd, rp, rlt, row_base, nra, ct, wa, wb)
    weigh(cp, clt, col_base, ncd, rp, rlt, row_base, nra, wt, wa, wb)

    def done(at, best):
        for tile in range(8):
            wt[tile, at, :] = jnp.minimum(wt[tile, at, :], best[tile])

    min_plus(xt, ct, 1, done)
    for t in range(8):
        o_ref[t * LANES : (t + 1) * LANES, :] = wt[t].T


def tile_of(base, rp, rl, cp, cl, pp, plists):
    rows, cols = rp.shape[0], cp.shape[0]

    def across(lists):
        return jnp.pad(lists.T, ((0, 16 - K), (0, 0)))

    vmem = pl.BlockSpec(memory_space=pltpu.VMEM)
    f32 = jnp.float32
    return pl.pallas_call(
        body,
        out_shape=jax.ShapeDtypeStruct((rows, cols), f32),
        in_specs=[pl.BlockSpec(memory_space=pltpu.SMEM)] + [vmem] * 6,
        out_specs=vmem,
        scratch_shapes=[
            pltpu.VMEM((rows // LANES, PB, LANES), f32),
            pltpu.VMEM((PB // LANES, cols, LANES), f32),
            pltpu.VMEM((PB // LANES, PB, LANES), f32),
            pltpu.VMEM((2 * FOLD, PB, LANES), f32),
            pltpu.VMEM((2 * FOLD, PB // FOLD, LANES), f32),
            pltpu.VMEM((PB // LANES, cols, LANES), f32),
            pltpu.VMEM((rows // LANES, cols, LANES), f32),
            pltpu.VMEM((rows // LANES, 8, LANES), f32),
            pltpu.VMEM((PB, LANES), f32),
            pltpu.VMEM((PB // LANES, 8, LANES), f32),
            pltpu.VMEM((cols, LANES), f32),
            pltpu.VMEM((PB, LANES), jnp.int32),
            pltpu.VMEM((rows // LANES, 8, LANES), jnp.int32),
        ],
        compiler_params=pltpu.CompilerParams(vmem_limit_bytes=40 << 20),
    )(base, rp, across(rl), cp, across(cl), pp, across(plists))


def local(features, neighbors, pivot):
    row_points, row_lists = (collect(features, "col", 0), collect(neighbors, "col", 0))
    row_count = row_points.shape[0]
    col_count = row_count * lax.axis_size("row") // lax.axis_size("col")
    row_index = lax.axis_index("row")
    col_index = lax.axis_index("col")
    offset = jnp.clip(col_index * col_count - row_index * row_count, 0, row_count - col_count)
    col_points = lax.dynamic_slice_in_dim(row_points, offset, col_count, 0)
    col_lists = lax.dynamic_slice_in_dim(row_lists, offset, col_count, 0)
    owner_row = col_index * col_count // row_count
    col_points, col_lists = (
        picked(col_points, "row", owner_row),
        picked(col_lists, "row", owner_row),
    )
    pivot_base = pivot[0] * PB
    pivot_row = pivot_base // row_count
    row_offset = jnp.clip(pivot_base - row_index * row_count, 0, row_count - PB)
    pivot_feats = lax.dynamic_slice_in_dim(row_points, row_offset, PB, 0)
    pivot_lists = lax.dynamic_slice_in_dim(row_lists, row_offset, PB, 0)
    pivot_feats, pivot_lists = (
        picked(pivot_feats, "row", pivot_row),
        picked(pivot_lists, "row", pivot_row),
    )
    base = jnp.stack([row_index * row_count, col_index * col_count, pivot_base]).astype(jnp.int32)
    return tile_of(base, row_points, row_lists, col_points, col_lists, pivot_feats, pivot_lists)


def solution(mesh):
    return jax.shard_map(
        local,
        mesh=mesh,
        in_specs=(P(("row", "col"), None), P(("row", "col"), None), P()),
        out_specs=P("row", "col"),
        check_vma=False,
    )
```

time: 249 us -> 245 us (0.984)
  Pallas kernels: 106 us -> 102 us
    pallas_call x1, Pallas kernels: 106 us -> 102 us  [tile_of(): pl.pallas_call(body, out_shape=jax.ShapeDtypeStruct((rows, cols), f32), i...]
where the time goes in v2:
time: 245 us; the launch traced here: 241 us
  Pallas kernels  102 us (42%)
  waiting for transfers between devices  52.7 us (22%)
  blocking collectives  46.9 us (19%)
  starting transfers between devices  17.6 us (7%)
  between operations  14.3 us (6%)
  local copies, waits for them, and re-layouts  6.49 us (3%)
    pallas_call x1, Pallas kernels, tile_of(): pl.pallas_call(body, out_shape=jax.ShapeDtypeStruct((rows, cols), f32), i...  102 us
    all_gather x2, blocking collectives, picked(): lax.all_gather(value, axis)  46.9 us
    all_to_all x2, waiting for transfers between devices, copy_for_each(): lax.all_to_all(jnp.broadcast_to(value[None], (size, *value.shape)), axis,...  37.6 us
    all_to_all x2, starting transfers between devices, copy_for_each(): lax.all_to_all(jnp.broadcast_to(value[None], (size, *value.shape)), axis,...  17.6 us
    all_gather x2, waiting for transfers between devices, picked(): lax.all_gather(value, axis)  14.4 us
  transfers between devices with their start and end apart: 4, of which 3 were waited for; matrix products, arithmetic and copies ran while one was open for 2% of the time, Pallas kernels for 0%

profile of v2, /device:TPU:1, one launch (start us, length us, event | category | flops | bytes accessed | tf_op | source)
XLA Modules:
  0.0 240.5 jit_solution(13336585944776706153)
XLA Ops:
  6.5 0.0 copy-start
  6.5 1.9 broadcast_in_dim.4
  8.4 12.7 %all-to-all-start = ((f32[32,32,256]{2,1,0:T(8,128)}), f32[32,32,256]{2,1,0:T(8,128)S(1)}, u32[]{:S(2)}, u32[]{:S(2)}) async-start(f32[32,32,256]{2,1,0:T(8,128)} %broadcast_in_dim.4), calls=%async_computation | async-start | bytes 2097152 | tf_op jit(solution)/shard_map/all_to_all | solution.py:19
  21.1 0.0 all-gather.7.cloned.1.call-start
  21.9 27.9 %all-to-all-done = f32[32,32,256]{2,1,0:T(8,128)S(1)} async-done(((f32[32,32,256]{2,1,0:T(8,128)}), f32[32,32,256]{2,1,0:T(8,128)S(1)}, u32[]{:S(2)}, u32[]{:S(2)}) %all-to-all-start) | async-done | bytes 1048608 | tf_op jit(solution)/shard_map/all_to_all | solution.py:19
  49.8 0.8 constant_dynamic-slice_fusion.2
  50.6 0.0 all-gather.7.cloned.1.call-update
  50.6 0.0 all-gather.9.cloned.1.call-start
  50.7 0.7 all-gather.9.cloned.1.call-update
  51.4 0.0 copy-done
  51.4 0.8 reshape.17
  52.2 4.8 %all-to-all-start.1 = ((s32[32,1,320]{2,1,0:T(1,128)}), s32[32,1,320]{2,1,0:T(1,128)S(1)}, u32[]{:S(2)}, u32[]{:S(2)}) async-start(s32[32,1,320]{2,1,0:T(1,128)} %reshape.17), calls=%async_computation.1 | async-start | bytes 98304 | tf_op jit(solution)/shard_map/all_to_all | solution.py:19
  57.0 0.1 pad_add_fusion.base
  57.1 9.7 %all-to-all-done.1 = s32[32,1,320]{2,1,0:T(1,128)S(1)} async-done(((s32[32,1,320]{2,1,0:T(1,128)}), s32[32,1,320]{2,1,0:T(1,128)S(1)}, u32[]{:S(2)}, u32[]{:S(2)}) %all-to-all-start.1) | async-done | bytes 40992 | tf_op jit(solution)/shard_map/all_to_all | solution.py:19
  66.8 0.6 broadcast.10
  67.4 0.7 reduce
  68.1 0.1 reshape.18
  68.2 0.1 copy.6
  68.3 0.1 reshape.12
  68.4 0.1 constant_dynamic-slice_fusion.1
  68.5 23.8 %all-gather.1 = s32[2048,10]{0,1:T(8,128)S(1)} all-gather(s32[256,10]{0,1:T(8,128)S(1)} %get-tuple-element.8), channel_id=3, replica_groups=mesh['row'=8,'col'=32] {'row'}, dimensions={0}, use_global_device_ids=true | all-gather | bytes 92160 | tf_op jit(solution)/shard_map/all_gather | solution.py:36
  92.4 23.1 %all-gather.3 = s32[2048,10]{0,1:T(8,128)S(1)} all-gather(s32[256,10]{0,1:T(8,128)S(1)} %get-tuple-element.7), channel_id=5, replica_groups=mesh['row'=8,'col'=32] {'row'}, dimensions={0}, use_global_device_ids=true | all-gather | bytes 92160 | tf_op jit(solution)/shard_map/all_gather | solution.py:36
  115.6 0.0 all-gather.7.cloned.1.call-done
  115.6 1.0 dynamic-slice_bitcast_fusion.1.cp
  116.6 14.3 %all-gather.9.cloned.1.call-done = f32[2048,256]{1,0:T(8,128)} async-done(((f32[256,256]{1,0:T(8,128)}), f32[2048,256]{1,0:T(8,128)}) %all-gather.9.cloned.1.call-update) | async-done | bytes 2097168 | tf_op jit(solution)/shard_map/all_gather | solution.py:36
  130.9 1.0 dynamic-slice_bitcast_fusion.pp
  131.9 101.8 %shard_map.37 = f32[1024,256]{1,0:T(8,128)} custom-call(s32[3]{0:T(128)S(1)} %pad_add_fusion.base, f32[1024,256]{1,0:T(8,128)S(1)} %bitcast.39, s32[16,1024]{1,0:T(8,128)S(1)} %pad.11.rlt, f32[256,256]{1,0:T(8,128)S(1)} %dynamic-slice_bitcast_fusion.1.cp, s32[16,256]{1,0:T(8,128)S(1)} %pad.12.clt, f32[256,256]{1,0:T(8,128)S(1)} %dynamic-slice_bitcast_fusion.pp, ...), custom_call_target="tpu_custom_call" | custom-call | tf_op jit(solution)/shard_map/pallas_call | solution.py:267
  (12 shorter events, 0.2 us)
Async XLA Ops:
  6.5 44.8 %copy-start = (s32[32,10]{0,1:T(8,128)S(1)}, s32[32,10]{0,1:T(8,128)}, u32[]{:S(2)}) copy-start(s32[32,10]{0,1:T(8,128)} %param.4) | copy-start | bytes 3844
  8.4 41.4 %all-to-all-start = ((f32[32,32,256]{2,1,0:T(8,128)}), f32[32,32,256]{2,1,0:T(8,128)S(1)}, u32[]{:S(2)}, u32[]{:S(2)}) async-start(f32[32,32,256]{2,1,0:T(8,128)} %broadcast_in_dim.4), calls=%async_computation | async-start | bytes 2097152 | tf_op jit(solution)/shard_map/all_to_all | solution.py:19
  21.1 94.5 %all-gather.7.cloned.1.call-start = ((), (), s32[]{:S(2)}) async-start(), calls=%async_computation.2 | async-start | bytes 2359296 | tf_op jit(solution)/shard_map/all_gather | solution.py:36
  50.6 80.3 %all-gather.9.cloned.1.call-start = ((), (), s32[]{:S(2)}) async-start(), calls=%async_computation.3 | async-start | bytes 2359296 | tf_op jit(solution)/shard_map/all_gather | solution.py:36
  52.2 14.6 %all-to-all-start.1 = ((s32[32,1,320]{2,1,0:T(1,128)}), s32[32,1,320]{2,1,0:T(1,128)S(1)}, u32[]{:S(2)}, u32[]{:S(2)}) async-start(s32[32,1,320]{2,1,0:T(1,128)} %reshape.17), calls=%async_computation.1 | async-start | bytes 98304 | tf_op jit(solution)/shard_map/all_to_all | solution.py:19
Sparse Core Ops, SparseCore 0:
  50.7 35.6 all-gather.6
  88.2 42.6 all-gather.8

commit v3 on v2

v3 whole, which is shorter than its diff:
```python
import functools

import jax
import jax.numpy as jnp
from jax import lax
from jax.experimental import pallas as pl
from jax.experimental.pallas import tpu as pltpu
from jax.sharding import PartitionSpec as P

MESH = pl.DeviceIdType.MESH
PB = 256
SQUARINGS = 3
K = 10
far_weight = 3.0
LANES = 128
SHARE = 32
PIECE = SHARE + 8
FOLD = 4
F32 = jnp.float32


def place():
    row, col = lax.axis_index("row"), lax.axis_index("col")
    return row, col, col // 8, lax.rem(col, 8) // 2, lax.rem(col, 2)


def send(src, dst, out_sem, in_sem, to):
    copy = pltpu.make_async_remote_copy(
        src_ref=src, dst_ref=dst, send_sem=out_sem, recv_sem=in_sem,
        device_id=to, device_id_type=MESH,
    )
    copy.start()
    return copy


def arrival(slot, out_sem, in_sem, to):
    pltpu.make_async_remote_copy(
        src_ref=slot, dst_ref=slot, send_sem=out_sem, recv_sem=in_sem,
        device_id=to, device_id_type=MESH,
    ).wait_recv()


def greet(row, col, y, m, home, whole):
    barrier = pltpu.get_barrier_semaphore()

    def signal(to):
        pl.semaphore_signal(barrier, inc=1, device_id=to, device_id_type=MESH)

    for d in range(1, 8):
        signal((lax.rem(row + d, 8), col))
        signal((row, y * 8 + lax.rem(m + d, 8)))
        signal((lax.rem(row + d, 8), home))
        signal((col // 4, lax.rem(col, 4) * 8 + lax.rem(m + d, 8)))
    for d in range(1, 4):
        signal((row, lax.rem(y + d, 4) * 8 + m))

    @pl.when(jnp.logical_not(whole))
    def _():
        signal((row, home))
        signal((col // 4, lax.rem(col, 4) * 8 + m))
        pl.semaphore_wait(barrier, 33)

    @pl.when(whole)
    def _():
        pl.semaphore_wait(barrier, 31)


def exchange(pivot, own, rows, cols, pivots, first, second,
             own_sem, s1, r1, s2, r2, s3, r3, sc, rc, sz, rz, sy, ry, sp, rp):
    row, col, y, zh, core = place()
    m = zh * 2 + core
    at = core * 4 + zh
    home = row * 4 + y
    whole = home == col
    mine = rows.at[y * 2 + core, zh]

    locals_ = [
        pltpu.make_async_copy(own, mine, own_sem.at[0]),
        pltpu.make_async_copy(own, first.at[row], own_sem.at[1]),
    ]
    for copy in locals_:
        copy.start()
    greet(row, col, y, m, home, whole)

    sent = []
    for d in range(1, 8):
        to = (lax.rem(row + d, 8), col)
        sent.append(send(own, first.at[row], s1.at[d], r1.at[row], to))
    for d in range(1, 4):
        to = (row, y * 8 + lax.rem(zh + d, 4) * 2 + core)
        sent.append(send(own, mine, sz.at[d], rz.at[zh], to))

    for d in range(1, 8):
        k = lax.rem(row + d, 8)
        arrival(first.at[k], s1.at[d], r1.at[k], (k, col))
    for copy in locals_:
        copy.wait()
    chosen = pivot[0] // 4
    second[y] = first[chosen]
    for d in range(1, 4):
        to = (row, lax.rem(y + d, 4) * 8 + m)
        sent.append(send(second.at[y], second.at[y], s2.at[d], r2.at[y], to))

    for d in range(8):
        to = (lax.rem(row + d, 8), home)
        if d:
            sent.append(send(own, cols.at[at], sc.at[d], rc.at[at], to))
    out = pltpu.make_async_remote_copy(
        src_ref=own, dst_ref=cols.at[at], send_sem=sc.at[0], recv_sem=rc.at[at],
        device_id=(row, home), device_id_type=MESH,
    )
    keep = pltpu.make_async_copy(own, cols.at[at], own_sem.at[2])

    @pl.when(whole)
    def _():
        keep.start()

    @pl.when(jnp.logical_not(whole))
    def _():
        out.start()

    for d in range(1, 4):
        k = lax.rem(y + d, 4)
        arrival(second.at[k], s2.at[d], r2.at[k], (row, k * 8 + m))
    pivots[at] = second[lax.rem(pivot[0], 4)]
    for d in range(1, 8):
        to = (row, y * 8 + lax.rem(m + d, 8))
        sent.append(send(pivots.at[at], pivots.at[at], s3.at[d], r3.at[at], to))

    for d in range(1, 4):
        k = lax.rem(zh + d, 4)
        arrival(rows.at[y * 2 + core, k], sz.at[d], rz.at[k], (row, y * 8 + k * 2 + core))
    share = rows.at[y * 2 + core]
    partner = (row, y * 8 + zh * 2 + 1 - core)
    for d in range(1, 4):
        to = (row, lax.rem(y + d, 4) * 8 + m)
        sent.append(send(share, share, sy.at[d], ry.at[y], to))
    sent.append(send(share, share, sp.at[0], rp.at[y], partner))

    for d in range(1, 8):
        k = lax.rem(m + d, 8)
        slot = lax.rem(k, 2) * 4 + k // 2
        arrival(pivots.at[slot], s3.at[d], r3.at[slot], (row, y * 8 + k))
    for d in range(1, 4):
        k = lax.rem(y + d, 4)
        share = rows.at[k * 2 + core]
        arrival(share, sy.at[d], ry.at[k], (row, k * 8 + m))
        sent.append(send(share, share, sp.at[d], rp.at[k], partner))
    for d in range(1, 8):
        k = lax.rem(m + d, 8)
        slot = lax.rem(k, 2) * 4 + k // 2
        arrival(cols.at[slot], sc.at[d], rc.at[slot], (col // 4, lax.rem(col, 4) * 8 + k))

    @pl.when(whole)
    def _():
        keep.wait()

    @pl.when(jnp.logical_not(whole))
    def _():
        out.wait_send()
        arrival(cols.at[at], sc.at[0], rc.at[at], (col // 4, lax.rem(col, 4) * 8 + m))

    for k in range(4):
        share = rows.at[k * 2 + 1 - core]
        arrival(share, sp.at[k], rp.at[k], partner)
    for copy in sent:
        copy.wait_send()


def moved(piece, pivot):
    sem = pltpu.SemaphoreType.DMA
    vmem = pl.BlockSpec(memory_space=pltpu.VMEM)
    return pl.pallas_call(
        exchange,
        out_shape=[
            jax.ShapeDtypeStruct((8, 4, PIECE, PB), F32),
            jax.ShapeDtypeStruct((8, PIECE, PB), F32),
            jax.ShapeDtypeStruct((8, PIECE, PB), F32),
        ],
        in_specs=[pl.BlockSpec(memory_space=pltpu.SMEM), vmem],
        out_specs=[vmem] * 3,
        scratch_shapes=[
            pltpu.VMEM((8, PIECE, PB), F32),
            pltpu.VMEM((4, PIECE, PB), F32),
            sem((3,)),
            sem((8,)), sem((8,)), sem((4,)), sem((4,)), sem((8,)), sem((8,)),
            sem((8,)), sem((8,)), sem((4,)), sem((4,)), sem((4,)), sem((4,)),
            sem((4,)), sem((4,)),
        ],
        compiler_params=pltpu.CompilerParams(
            collective_id=0, has_side_effects=True, vmem_limit_bytes=16 << 20
        ),
    )(pivot, piece)


def dot(a, b, dims):
    return lax.dot_general(
        a, b, (dims, ((), ())),
        precision=lax.Precision.HIGHEST, preferred_element_type=F32,
    )


def points_of(pieces, tile):
    return pieces[tile, :, :SHARE, :].reshape(LANES, PB)


def lists_of(pieces, tile):
    both = pieces[tile, 0, SHARE:, :]
    for zh in range(1, 4):
        both = both + pieces[tile, zh, SHARE:, :]
    both = both.astype(jnp.int32)
    return jnp.concatenate([both[:, :LANES], both[:, LANES:]], axis=0)


def norms_down(points, out):
    for tile in range(2):
        p = points_of(points, tile)
        out[tile * LANES : (tile + 1) * LANES, :] = dot(
            p * p, jnp.ones((PB, LANES), F32), ((1,), (0,))
        )


def norms_across(points, out):
    def chunk(t, carry):
        p = points_of(points, t)
        out[t] = dot(jnp.ones((8, PB), F32), p * p, ((1,), (1,)))
        return carry

    lax.fori_loop(0, points.shape[0], chunk, 0)


def bits_of(lists, base, words):
    word = lax.broadcasted_iota(jnp.int32, (words, LANES), 0)
    found = jnp.zeros((words, LANES), jnp.int32)
    for slot in range(K):
        at = lists[slot : slot + 1, :] - base
        bit = jnp.left_shift(jnp.int32(1), at & 31)
        found = found | jnp.where(jnp.right_shift(at, 5) == word, bit, 0)
    return found


def lanes_of(piece, index):
    dims = lax.GatherDimensionNumbers(
        offset_dims=(), collapsed_slice_dims=(1,), start_index_map=(1,),
        operand_batching_dims=(0,), start_indices_batching_dims=(0,),
    )
    return lax.gather(
        piece, index[:, :, None], dims, (1, 1), mode=lax.GatherScatterMode.PROMISE_IN_BOUNDS
    )


def weigh(down_of, base_a, norm_a, across_of, base_b, norm_b, out, wa, wb):
    tiles = across_of.shape[0]
    for tile in range(2):
        bits = bits_of(lists_of(down_of, tile), base_b, 4 * tiles)
        pad = jnp.zeros((LANES - 4 * tiles, LANES), jnp.int32)
        wa[tile * LANES : (tile + 1) * LANES, :] = jnp.concatenate([bits, pad], axis=0).T

    def words(t, carry):
        wb[t] = bits_of(lists_of(across_of, t), base_a, 8)
        return carry

    lax.fori_loop(0, tiles, words, 0)
    a = jnp.concatenate([points_of(down_of, 0), points_of(down_of, 1)], axis=0)

    def products(t, carry):
        b = jnp.concatenate([points_of(across_of, 2 * t), points_of(across_of, 2 * t + 1)], axis=0)
        inner = dot(a, b, ((1,), (1,)))
        out[2 * t] = inner[:, :LANES]
        out[2 * t + 1] = inner[:, LANES:]
        return carry

    lax.fori_loop(0, tiles // 2, products, 0)

    lane = lax.broadcasted_iota(jnp.int32, (32, LANES), 1)
    inside = lane & 31
    across = (lane // 32) * 64 + inside
    down = lax.broadcasted_iota(jnp.int32, (32, LANES), 0)

    def group(n, carry):
        t, g = n // 8, n % 8
        rows = pl.ds(pl.multiple_of(g * 32, 32), 32)
        word_a = (t // 2) * 8 + t % 2
        word_b = (g % 4) * 2 + g // 4
        squares = norm_a[rows, :] + jnp.tile(norm_b[t], (4, 1)) - 2.0 * out[t, rows, :]
        squares = jnp.maximum(squares, 0.0)
        length = squares * lax.rsqrt(jnp.maximum(squares, 1.2e-38))
        listed = lanes_of(wa[rows, :], (lane // 32) * 2 + word_a)
        listed = jnp.right_shift(listed, inside)
        lists = jnp.tile(wb[t, pl.ds(word_b, 8, stride=0), :], (4, 1))
        listed = listed | jnp.right_shift(lists, down)
        weighted = jnp.where((listed & 1) == 1, length, far_weight * length)
        same = (down - across) == (base_b - base_a + 32 * (word_a - word_b))
        out[t, rows, :] = jnp.where(same, 0.0, weighted)
        return carry

    lax.fori_loop(0, tiles * 8, group, 0)


def min_plus(left, right, fold, done, rows):
    tiles = right.shape[0]
    halves = left.shape[0]
    depth = right.shape[1] // halves
    subs = rows // 8
    pattern = lax.broadcasted_iota(jnp.int32, (8, LANES), 1) // (LANES // fold)

    def block(t, carry):
        def rows_of(s):
            return pl.ds(pl.multiple_of(t * rows + 8 * s, 8), 8)

        def half(h, best):
            best = list(best)
            pieces = [left[h, rows_of(s), :] for s in range(subs)]
            for q in range(depth):
                downs = [lanes_of(piece, pattern + q * fold) for piece in pieces]
                for tile in range(tiles):
                    row = right[tile, pl.ds(h * depth + q, 8, stride=0), :]
                    for s in range(subs):
                        n = tile * subs + s
                        best[n] = jnp.minimum(best[n], downs[s] + row)
            return tuple(best)

        best = tuple(jnp.full((8, LANES), jnp.inf, F32) for _ in range(tiles * subs))
        best = lax.fori_loop(0, halves, half, best)
        for s in range(subs):
            done(rows_of(s), [best[tile * subs + s] for tile in range(tiles)])
        return carry

    lax.fori_loop(0, left.shape[1] // rows, block, 0)


def folded(wide, right):
    lane = lax.broadcasted_iota(jnp.int32, (PB // FOLD, LANES), 1) // (LANES // FOLD)
    for tile in range(wide.shape[0]):
        piece = wide[tile, pl.ds(0, PB // FOLD, stride=FOLD), :]
        for c in range(1, FOLD):
            other = wide[tile, pl.ds(c, PB // FOLD, stride=FOLD), :]
            piece = jnp.where(lane == c, other, piece)
        right[tile] = piece


def gathered(parts):
    group = lax.broadcasted_iota(jnp.int32, parts[0].shape, 1) // (LANES // FOLD)
    tile = parts[0]
    for c in range(1, FOLD):
        tile = jnp.where(group == c, parts[c], tile)
    return tile


def reduced(piece):
    piece = jnp.minimum(piece, pltpu.roll(piece, 64, 1))
    return jnp.minimum(piece, pltpu.roll(piece, 32, 1))


def spread(tiles, wide):
    lane = lax.broadcasted_iota(jnp.int32, (32, LANES), 1) % (LANES // FOLD)
    for g in range(wide.shape[0]):

        def chunk(t, carry):
            rows = pl.ds(pl.multiple_of(t * 32, 32), 32)
            piece = tiles[g // FOLD, rows, :]
            wide[g, rows, :] = lanes_of(piece, lane + 32 * (g % FOLD))
            return carry

        lax.fori_loop(0, PB // 32, chunk, 0)


def body(base, rb, cb, pb, o_ref, ct, bt, ka, wide, fold, xt, wt, nra, npd, npa, ncd, wa, wb):
    row_base, col_base, pivot_base = base[0], base[1], base[2]
    norms_across(rb, nra)
    norms_across(pb, npa)
    norms_down(pb, npd)
    norms_down(cb, ncd)
    weigh(pb, pivot_base, npd, pb, pivot_base, npa, ka, wa, wb)
    spread(ka, wide)

    def square(turn, carry):
        folded(wide, fold)

        def done(at, best):
            best = [reduced(b) for b in best]
            for g in range(8):
                wide[g, at, :] = best[g]
            for tile in range(2):
                kept = gathered(best[FOLD * tile : FOLD * tile + FOLD])
                ka[tile, at, :] = jnp.minimum(ka[tile, at, :], kept)

        min_plus(ka, fold, FOLD, done, 32)
        return carry

    lax.fori_loop(0, SQUARINGS + 1, square, 0)
    folded(wide, fold)
    weigh(cb, col_base, ncd, pb, pivot_base, npa, bt, wa, wb)

    def done(at, best):
        best = [reduced(b) for b in best]
        for tile in range(2):
            kept = gathered(best[FOLD * tile : FOLD * tile + FOLD])
            xt[tile, at, :] = jnp.minimum(bt[tile, at, :], kept)

    min_plus(bt, fold, FOLD, done, 32)
    weigh(pb, pivot_base, npd, rb, row_base, nra, ct, wa, wb)
    weigh(cb, col_base, ncd, rb, row_base, nra, wt, wa, wb)

    def done(at, best):
        for tile in range(8):
            wt[tile, at, :] = jnp.minimum(wt[tile, at, :], best[tile])

    min_plus(xt, ct, 1, done, 32)
    for t in range(8):
        for n in range(2):
            parts = [
                wt[t, (m % 2) * LANES + (m // 2) * 32 : (m % 2) * LANES + (m // 2) * 32 + 32, :]
                for m in range(4 * n, 4 * n + 4)
            ]
            flat = jnp.concatenate(parts, axis=0).T
            for zh in range(4):
                top = (t // 2) * 256 + (2 * zh + t % 2) * 32
                o_ref[top : top + 32, n * LANES : (n + 1) * LANES] = flat[zh * 32 : zh * 32 + 32]


def tile_of(base, rows, cols, pivots):
    vmem = pl.BlockSpec(memory_space=pltpu.VMEM)
    tiles = rows.shape[0]
    return pl.pallas_call(
        body,
        out_shape=jax.ShapeDtypeStruct((tiles * LANES, PB), F32),
        in_specs=[pl.BlockSpec(memory_space=pltpu.SMEM)] + [vmem] * 3,
        out_specs=vmem,
        scratch_shapes=[
            pltpu.VMEM((tiles, PB, LANES), F32),
            pltpu.VMEM((2, PB, LANES), F32),
            pltpu.VMEM((2, PB, LANES), F32),
            pltpu.VMEM((2 * FOLD, PB, LANES), F32),
            pltpu.VMEM((2 * FOLD, PB // FOLD, LANES), F32),
            pltpu.VMEM((2, PB, LANES), F32),
            pltpu.VMEM((tiles, PB, LANES), F32),
            pltpu.VMEM((tiles, 8, LANES), F32),
            pltpu.VMEM((PB, LANES), F32),
            pltpu.VMEM((2, 8, LANES), F32),
            pltpu.VMEM((PB, LANES), F32),
            pltpu.VMEM((PB, LANES), jnp.int32),
            pltpu.VMEM((tiles, 8, LANES), jnp.int32),
        ],
        compiler_params=pltpu.CompilerParams(vmem_limit_bytes=40 << 20),
    )(base, rows, cols, pivots)


def local(features, neighbors, pivot):
    row, col, y, zh, core = place()
    lists = jnp.zeros((16, LANES), F32)
    lists = lax.dynamic_update_slice(lists, neighbors.T.astype(F32), (0, zh * SHARE))
    lists = jnp.concatenate([lists[:8], lists[8:]], axis=1)
    piece = jnp.concatenate([features, lists], axis=0)
    rows, cols, pivots = moved(piece, pivot)
    base = jnp.stack([row * 1024, col * PB, pivot[0] * PB]).astype(jnp.int32)
    return tile_of(
        base, rows, cols.reshape(2, 4, PIECE, PB), pivots.reshape(2, 4, PIECE, PB)
    )


def solution(mesh):
    return jax.shard_map(
        local,
        mesh=mesh,
        in_specs=(P(("row", "col"), None), P(("row", "col"), None), P()),
        out_specs=P("row", "col"),
        check_vma=False,
    )
```

time: 245 us -> 138 us (0.56); the launches traced: 241 us -> 138 us
  waiting for transfers between devices: 52.7 us -> 0 us
  blocking collectives: 46.9 us -> 0 us
  Pallas kernels: 102 us -> 136 us
  starting transfers between devices: 17.6 us -> 0 us
  between operations: 14.3 us -> 0.68 us
  local copies, waits for them, and re-layouts: 6.49 us -> 0.31 us
    all_gather x2 -> x0, blocking collectives: 46.9 us -> none  [picked(): lax.all_gather(value, axis)]
    all_to_all x2 -> x0, waiting for transfers between devices: 37.6 us -> none  [copy_for_each(): lax.all_to_all(jnp.broadcast_to(value[None], (size, *value.shape)), axis,...]
    pallas_call x1 -> x2, Pallas kernels: 102 us -> 136 us  [the longest x1 85 us: tile_of(): pl.pallas_call(body, out_shape=jax.ShapeDtypeStruct((tiles * LANES, PB),...]
    all_to_all x2 -> x0, starting transfers between devices: 17.6 us -> none  [copy_for_each(): lax.all_to_all(jnp.broadcast_to(value[None], (size, *value.shape)), axis,...]
    all_gather x2 -> x0, waiting for transfers between devices: 14.4 us -> none  [picked(): lax.all_gather(value, axis)]
  transfers between devices with their start and end apart: 4 -> 0, of which waited for: 3 -> 0; matrix products, arithmetic and copies ran while one was open for 2% -> 0% of each run, Pallas kernels for 0% -> 0%
where the time goes in v3:
time: 138 us
  Pallas kernels  136 us (99%)
  other arithmetic  1.54 us (1%)
    pallas_call x1, Pallas kernels, tile_of(): pl.pallas_call(body, out_shape=jax.ShapeDtypeStruct((tiles * LANES, PB),...  85 us
    pallas_call x1, Pallas kernels, moved(): pl.pallas_call(exchange, out_shape=[jax.ShapeDtypeStruct((8, 4, PIECE, PB...  50.5 us

profile of v3, /device:TPU:1, one launch (start us, length us, event | category | flops | bytes accessed | tf_op | source)
XLA Modules:
  0.0 138.1 jit_solution(3837286183608331741)
XLA Ops:
  0.7 0.1 pad_add_fusion.base
  0.7 0.7 convert_bitcast_fusion
  1.4 0.3 dynamic_update_slice.3
  1.8 0.8 maximum_maximum_fusion.own
  2.5 50.5 %shard_map.37 = (f32[8,4,40,256]{3,2,1,0:T(8,128)S(1)}, f32[8,40,256]{2,1,0:T(8,128)S(1)}, f32[8,40,256]{2,1,0:T(8,128)S(1)}) custom-call(s32[1]{0:T(128)S(6)} %copy.5.pivot, f32[40,256]{1,0:T(8,128)S(1)} %maximum_maximum_fusion.own), custom_call_target="tpu_custom_call" | custom-call | tf_op jit(solution)/shard_map/pallas_call | solution.py:173
  53.1 85.0 %shard_map.38 = f32[1024,256]{1,0:T(8,128)} custom-call(s32[3]{0:T(128)S(1)} %pad_add_fusion.base, f32[8,4,40,256]{3,2,1,0:T(8,128)S(1)} %get-tuple-element.8.rb, f32[2,4,40,256]{3,2,1,0:T(8,128)S(1)} %bitcast.6, f32[2,4,40,256]{3,2,1,0:T(8,128)S(1)} %bitcast.7), custom_call_target="tpu_custom_call" | custom-call | tf_op jit(solution)/shard_map/pallas_call | solution.py:425
  (2 shorter events, 0.0 us)

commit v4 on v3

--- a/solution.py
+++ b/solution.py
@@ -40,7 +40,7 @@
     ).wait_recv()
 
 
-def greet(row, col, y, m, home, whole):
+def greet(row, col, y, m):
     barrier = pltpu.get_barrier_semaphore()
 
     def signal(to):
@@ -49,38 +49,28 @@
     for d in range(1, 8):
         signal((lax.rem(row + d, 8), col))
         signal((row, y * 8 + lax.rem(m + d, 8)))
-        signal((lax.rem(row + d, 8), home))
-        signal((col // 4, lax.rem(col, 4) * 8 + lax.rem(m + d, 8)))
     for d in range(1, 4):
         signal((row, lax.rem(y + d, 4) * 8 + m))
-
-    @pl.when(jnp.logical_not(whole))
-    def _():
-        signal((row, home))
-        signal((col // 4, lax.rem(col, 4) * 8 + m))
-        pl.semaphore_wait(barrier, 33)
-
-    @pl.when(whole)
-    def _():
-        pl.semaphore_wait(barrier, 31)
-
-
-def exchange(pivot, own, rows, cols, pivots, first, second,
-             own_sem, s1, r1, s2, r2, s3, r3, sc, rc, sz, rz, sy, ry, sp, rp):
+    pl.semaphore_wait(barrier, 17)
+
+
+def gather_and_close(pivot, own, rows, cols, pivots, closed, first, second, ka, wide, fold,
+                     npd, npa, wa, wb, own_sem, s1, r1, s2, r2, s3, r3, s4, r4,
+                     sc, rc, sz, rz, sy, ry, sp, rp, sf, rf):
     row, col, y, zh, core = place()
     m = zh * 2 + core
-    at = core * 4 + zh
     home = row * 4 + y
     whole = home == col
     mine = rows.at[y * 2 + core, zh]
-
-    locals_ = [
+    partner = (row, y * 8 + zh * 2 + 1 - core)
+
+    kept = [
         pltpu.make_async_copy(own, mine, own_sem.at[0]),
         pltpu.make_async_copy(own, first.at[row], own_sem.at[1]),
     ]
-    for copy in locals_:
+    for copy in kept:
         copy.start()
-    greet(row, col, y, m, home, whole)
+    greet(row, col, y, m)
 
     sent = []
     for d in range(1, 8):
@@ -89,27 +79,47 @@
     for d in range(1, 4):
         to = (row, y * 8 + lax.rem(zh + d, 4) * 2 + core)
         sent.append(send(own, mine, sz.at[d], rz.at[zh], to))
-
     for d in range(1, 8):
         k = lax.rem(row + d, 8)
         arrival(first.at[k], s1.at[d], r1.at[k], (k, col))
-    for copy in locals_:
+    for copy in kept:
         copy.wait()
-    chosen = pivot[0] // 4
-    second[y] = first[chosen]
+    second[y] = first[pivot[0] // 4]
     for d in range(1, 4):
         to = (row, lax.rem(y + d, 4) * 8 + m)
         sent.append(send(second.at[y], second.at[y], s2.at[d], r2.at[y], to))
-
-    for d in range(8):
+    for d in range(1, 4):
+        k = lax.rem(y + d, 4)
+        arrival(second.at[k], s2.at[d], r2.at[k], (row, k * 8 + m))
+    pivots[core, zh] = second[lax.rem(pivot[0], 4)]
+    piece = pivots.at[core, zh]
+    for d in range(1, 4):
+        to = (row, y * 8 + lax.rem(zh + d, 4) * 2 + core)
+        sent.append(send(piece, piece, s3.at[d], r3.at[zh], to))
+
+    for d in range(1, 4):
+        k = lax.rem(zh + d, 4)
+        arrival(rows.at[y * 2 + core, k], sz.at[d], rz.at[k], (row, y * 8 + k * 2 + core))
+    share = rows.at[y * 2 + core]
+    for d in range(1, 4):
+        to = (row, lax.rem(y + d, 4) * 8 + m)
+        sent.append(send(share, share, sy.at[d], ry.at[y], to))
+
+    for d in range(1, 4):
+        k = lax.rem(zh + d, 4)
+        arrival(pivots.at[core, k], s3.at[d], r3.at[k], (row, y * 8 + k * 2 + core))
+    sent.append(send(pivots.at[core], pivots.at[core], s4.at[0], r4.at[0], partner))
+    sent.append(send(share, share, sp.at[0], rp.at[y], partner))
+    arrival(pivots.at[1 - core], s4.at[0], r4.at[0], partner)
+
+    for d in range(1, 8):
         to = (lax.rem(row + d, 8), home)
-        if d:
-            sent.append(send(own, cols.at[at], sc.at[d], rc.at[at], to))
+        sent.append(send(own, cols.at[core, zh], sc.at[d], rc.at[m], to))
     out = pltpu.make_async_remote_copy(
-        src_ref=own, dst_ref=cols.at[at], send_sem=sc.at[0], recv_sem=rc.at[at],
+        src_ref=own, dst_ref=cols.at[core, zh], send_sem=sc.at[0], recv_sem=rc.at[m],
         device_id=(row, home), device_id_type=MESH,
     )
-    keep = pltpu.make_async_copy(own, cols.at[at], own_sem.at[2])
+    keep = pltpu.make_async_copy(own, cols.at[core, zh], own_sem.at[2])
 
     @pl.when(whole)
     def _():
@@ -119,37 +129,49 @@
     def _():
         out.start()
 
-    for d in range(1, 4):
-        k = lax.rem(y + d, 4)
-        arrival(second.at[k], s2.at[d], r2.at[k], (row, k * 8 + m))
-    pivots[at] = second[lax.rem(pivot[0], 4)]
-    for d in range(1, 8):
-        to = (row, y * 8 + lax.rem(m + d, 8))
-        sent.append(send(pivots.at[at], pivots.at[at], s3.at[d], r3.at[at], to))
-
-    for d in range(1, 4):
-        k = lax.rem(zh + d, 4)
-        arrival(rows.at[y * 2 + core, k], sz.at[d], rz.at[k], (row, y * 8 + k * 2 + core))
-    share = rows.at[y * 2 + core]
-    partner = (row, y * 8 + zh * 2 + 1 - core)
-    for d in range(1, 4):
-        to = (row, lax.rem(y + d, 4) * 8 + m)
-        sent.append(send(share, share, sy.at[d], ry.at[y], to))
-    sent.append(send(share, share, sp.at[0], rp.at[y], partner))
-
-    for d in range(1, 8):
-        k = lax.rem(m + d, 8)
-        slot = lax.rem(k, 2) * 4 + k // 2
-        arrival(pivots.at[slot], s3.at[d], r3.at[slot], (row, y * 8 + k))
+    base = pivot[0] * PB
+    norms_across(pivots, npa)
+    norms_down(pivots, npd)
+    weigh(pivots, base, npd, pivots, base, npa, ka, wa, wb)
+    spread(ka, wide)
+    folded(wide, fold.at[0], 0, PB // FOLD)
+    top = core * LANES
+
+    def square(turn, carry):
+        old, new = lax.rem(turn, 2), lax.rem(turn + 1, 2)
+
+        def done(at, best):
+            best = [reduced(b) for b in best]
+            for g in range(2 * FOLD):
+                wide[g, at, :] = best[g]
+            for tile in range(2):
+                part = gathered(best[FOLD * tile : FOLD * tile + FOLD])
+                ka[tile, at, :] = jnp.minimum(ka[tile, at, :], part)
+
+        min_plus(ka, fold.at[old], FOLD, done, 32, top, LANES)
+        half = LANES // FOLD
+        low = pl.multiple_of(core * half, half)
+        folded(wide.at[:, pl.ds(pl.multiple_of(top, LANES), LANES)], fold.at[new], low, half)
+        ours = fold.at[new, :, pl.ds(low, half)]
+        theirs = fold.at[new, :, pl.ds(pl.multiple_of(half - low, half), half)]
+        copy = send(ours, ours, sf.at[new], rf.at[new], partner)
+        arrival(theirs, sf.at[new], rf.at[new], partner)
+        copy.wait_send()
+        return carry
+
+    lax.fori_loop(0, 1, square, 0)
     for d in range(1, 4):
         k = lax.rem(y + d, 4)
         share = rows.at[k * 2 + core]
         arrival(share, sy.at[d], ry.at[k], (row, k * 8 + m))
         sent.append(send(share, share, sp.at[d], rp.at[k], partner))
+    lax.fori_loop(1, SQUARINGS + 1, square, 0)
+    closed[...] = fold[(SQUARINGS + 1) % 2]
+
     for d in range(1, 8):
         k = lax.rem(m + d, 8)
-        slot = lax.rem(k, 2) * 4 + k // 2
-        arrival(cols.at[slot], sc.at[d], rc.at[slot], (col // 4, lax.rem(col, 4) * 8 + k))
+        slot = cols.at[lax.rem(k, 2), k // 2]
+        arrival(slot, sc.at[d], rc.at[k], (col // 4, lax.rem(col, 4) * 8 + k))
 
     @pl.when(whole)
     def _():
@@ -158,11 +180,14 @@
     @pl.when(jnp.logical_not(whole))
     def _():
         out.wait_send()
-        arrival(cols.at[at], sc.at[0], rc.at[at], (col // 4, lax.rem(col, 4) * 8 + m))
 
     for k in range(4):
-        share = rows.at[k * 2 + 1 - core]
-        arrival(share, sp.at[k], rp.at[k], partner)
+        arrival(rows.at[k * 2 + 1 - core], sp.at[k], rp.at[k], partner)
+
+    @pl.when(jnp.logical_not(whole))
+    def _():
+        arrival(cols.at[core, zh], sc.at[0], rc.at[m], (col // 4, lax.rem(col, 4) * 8 + m))
+
     for copy in sent:
         copy.wait_send()
 
@@ -171,24 +196,32 @@
     sem = pltpu.SemaphoreType.DMA
     vmem = pl.BlockSpec(memory_space=pltpu.VMEM)
     return pl.pallas_call(
-        exchange,
+        gather_and_close,
         out_shape=[
             jax.ShapeDtypeStruct((8, 4, PIECE, PB), F32),
-            jax.ShapeDtypeStruct((8, PIECE, PB), F32),
-            jax.ShapeDtypeStruct((8, PIECE, PB), F32),
+            jax.ShapeDtypeStruct((2, 4, PIECE, PB), F32),
+            jax.ShapeDtypeStruct((2, 4, PIECE, PB), F32),
+            jax.ShapeDtypeStruct((2 * FOLD, PB // FOLD, LANES), F32),
         ],
         in_specs=[pl.BlockSpec(memory_space=pltpu.SMEM), vmem],
-        out_specs=[vmem] * 3,
+        out_specs=[vmem] * 4,
         scratch_shapes=[
             pltpu.VMEM((8, PIECE, PB), F32),
             pltpu.VMEM((4, PIECE, PB), F32),
+            pltpu.VMEM((2, PB, LANES), F32),
+            pltpu.VMEM((2 * FOLD, PB, LANES), F32),
+            pltpu.VMEM((2, 2 * FOLD, PB // FOLD, LANES), F32),
+            pltpu.VMEM((PB, LANES), F32),
+            pltpu.VMEM((2, 8, LANES), F32),
+            pltpu.VMEM((PB, LANES), jnp.int32),
+            pltpu.VMEM((2, 8, LANES), jnp.int32),
             sem((3,)),
-            sem((8,)), sem((8,)), sem((4,)), sem((4,)), sem((8,)), sem((8,)),
+            sem((8,)), sem((8,)), sem((4,)), sem((4,)), sem((4,)), sem((4,)), sem((1,)), sem((1,)),
             sem((8,)), sem((8,)), sem((4,)), sem((4,)), sem((4,)), sem((4,)),
-            sem((4,)), sem((4,)),
+            sem((4,)), sem((4,)), sem((2,)), sem((2,)),
         ],
         compiler_params=pltpu.CompilerParams(
-            collective_id=0, has_side_effects=True, vmem_limit_bytes=16 << 20
+            collective_id=0, has_side_effects=True, vmem_limit_bytes=24 << 20
         ),
     )(pivot, piece)
 
@@ -297,7 +330,7 @@
     lax.fori_loop(0, tiles * 8, group, 0)
 
 
-def min_plus(left, right, fold, done, rows):
+def min_plus(left, right, fold, done, rows, top, count):
     tiles = right.shape[0]
     halves = left.shape[0]
     depth = right.shape[1] // halves
@@ -306,7 +339,7 @@
 
     def block(t, carry):
         def rows_of(s):
-            return pl.ds(pl.multiple_of(t * rows + 8 * s, 8), 8)
+            return pl.ds(pl.multiple_of(top + t * rows + 8 * s, 8), 8)
 
         def half(h, best):
             best = list(best)
@@ -326,17 +359,17 @@
             done(rows_of(s), [best[tile * subs + s] for tile in range(tiles)])
         return carry
 
-    lax.fori_loop(0, left.shape[1] // rows, block, 0)
-
-
-def folded(wide, right):
-    lane = lax.broadcasted_iota(jnp.int32, (PB // FOLD, LANES), 1) // (LANES // FOLD)
+    lax.fori_loop(0, count // rows, block, 0)
+
+
+def folded(wide, right, low, count):
+    lane = lax.broadcasted_iota(jnp.int32, (count, LANES), 1) // (LANES // FOLD)
     for tile in range(wide.shape[0]):
-        piece = wide[tile, pl.ds(0, PB // FOLD, stride=FOLD), :]
+        piece = wide[tile, pl.ds(0, count, stride=FOLD), :]
         for c in range(1, FOLD):
-            other = wide[tile, pl.ds(c, PB // FOLD, stride=FOLD), :]
+            other = wide[tile, pl.ds(c, count, stride=FOLD), :]
             piece = jnp.where(lane == c, other, piece)
-        right[tile] = piece
+        right[tile, pl.ds(low, count), :] = piece
 
 
 def gathered(parts):
@@ -353,43 +386,23 @@
 
 
 def spread(tiles, wide):
-    lane = lax.broadcasted_iota(jnp.int32, (32, LANES), 1) % (LANES // FOLD)
-    for g in range(wide.shape[0]):
-
-        def chunk(t, carry):
-            rows = pl.ds(pl.multiple_of(t * 32, 32), 32)
-            piece = tiles[g // FOLD, rows, :]
-            wide[g, rows, :] = lanes_of(piece, lane + 32 * (g % FOLD))
-            return carry
-
-        lax.fori_loop(0, PB // 32, chunk, 0)
-
-
-def body(base, rb, cb, pb, o_ref, ct, bt, ka, wide, fold, xt, wt, nra, npd, npa, ncd, wa, wb):
+    lane = lax.broadcasted_iota(jnp.int32, (32, LANES), 1) & 31
+
+    def chunk(t, carry):
+        rows = pl.ds(pl.multiple_of(t * 32, 32), 32)
+        for g in range(wide.shape[0]):
+            wide[g, rows, :] = lanes_of(tiles[g // FOLD, rows, :], lane + 32 * (g % FOLD))
+        return carry
+
+    lax.fori_loop(0, PB // 32, chunk, 0)
+
+
+def body(base, rb, cb, pb, fold, o_ref, ct, bt, xt, wt, nra, npd, npa, ncd, wa, wb):
     row_base, col_base, pivot_base = base[0], base[1], base[2]
     norms_across(rb, nra)
     norms_across(pb, npa)
     norms_down(pb, npd)
     norms_down(cb, ncd)
-    weigh(pb, pivot_base, npd, pb, pivot_base, npa, ka, wa, wb)
-    spread(ka, wide)
-
-    def square(turn, carry):
-        folded(wide, fold)
-
-        def done(at, best):
-            best = [reduced(b) for b in best]
-            for g in range(8):
-                wide[g, at, :] = best[g]
-            for tile in range(2):
-                kept = gathered(best[FOLD * tile : FOLD * tile + FOLD])
-                ka[tile, at, :] = jnp.minimum(ka[tile, at, :], kept)
-
-        min_plus(ka, fold, FOLD, done, 32)
-        return carry
-
-    lax.fori_loop(0, SQUARINGS + 1, square, 0)
-    folded(wide, fold)
     weigh(cb, col_base, ncd, pb, pivot_base, npa, bt, wa, wb)
 
     def done(at, best):
@@ -398,7 +411,7 @@
             kept = gathered(best[FOLD * tile : FOLD * tile + FOLD])
             xt[tile, at, :] = jnp.minimum(bt[tile, at, :], kept)
 
-    min_plus(bt, fold, FOLD, done, 32)
+    min_plus(bt, fold, FOLD, done, 32, 0, PB)
     weigh(pb, pivot_base, npd, rb, row_base, nra, ct, wa, wb)
     weigh(cb, col_base, ncd, rb, row_base, nra, wt, wa, wb)
 
@@ -406,7 +419,7 @@
         for tile in range(8):
             wt[tile, at, :] = jnp.minimum(wt[tile, at, :], best[tile])
 
-    min_plus(xt, ct, 1, done, 32)
+    min_plus(xt, ct, 1, done, 32, 0, PB)
     for t in range(8):
         for n in range(2):
             parts = [
@@ -419,20 +432,17 @@
                 o_ref[top : top + 32, n * LANES : (n + 1) * LANES] = flat[zh * 32 : zh * 32 + 32]
 
 
-def tile_of(base, rows, cols, pivots):
+def tile_of(base, rows, cols, pivots, closed):
     vmem = pl.BlockSpec(memory_space=pltpu.VMEM)
     tiles = rows.shape[0]
     return pl.pallas_call(
         body,
         out_shape=jax.ShapeDtypeStruct((tiles * LANES, PB), F32),
-        in_specs=[pl.BlockSpec(memory_space=pltpu.SMEM)] + [vmem] * 3,
+        in_specs=[pl.BlockSpec(memory_space=pltpu.SMEM)] + [vmem] * 4,
         out_specs=vmem,
         scratch_shapes=[
             pltpu.VMEM((tiles, PB, LANES), F32),
             pltpu.VMEM((2, PB, LANES), F32),
-            pltpu.VMEM((2, PB, LANES), F32),
-            pltpu.VMEM((2 * FOLD, PB, LANES), F32),
-            pltpu.VMEM((2 * FOLD, PB // FOLD, LANES), F32),
             pltpu.VMEM((2, PB, LANES), F32),
             pltpu.VMEM((tiles, PB, LANES), F32),
             pltpu.VMEM((tiles, 8, LANES), F32),
@@ -443,7 +453,7 @@
             pltpu.VMEM((tiles, 8, LANES), jnp.int32),
         ],
         compiler_params=pltpu.CompilerParams(vmem_limit_bytes=40 << 20),
-    )(base, rows, cols, pivots)
+    )(base, rows, cols, pivots, closed)
 
 
 def local(features, neighbors, pivot):
@@ -452,11 +462,9 @@
     lists = lax.dynamic_update_slice(lists, neighbors.T.astype(F32), (0, zh * SHARE))
     lists = jnp.concatenate([lists[:8], lists[8:]], axis=1)
     piece = jnp.concatenate([features, lists], axis=0)
-    rows, cols, pivots = moved(piece, pivot)
+    rows, cols, pivots, closed = moved(piece, pivot)
     base = jnp.stack([row * 1024, col * PB, pivot[0] * PB]).astype(jnp.int32)
-    return tile_of(
-        base, rows, cols.reshape(2, 4, PIECE, PB), pivots.reshape(2, 4, PIECE, PB)
-    )
+    return tile_of(base, rows, cols, pivots, closed)
 
 
 def solution(mesh):

time: 138 us -> 103 us (0.75); the launches traced: 138 us -> 101 us
  Pallas kernels: 136 us -> 98.9 us
    pallas_call x1, Pallas kernels: 85 us -> 48.4 us  [tile_of(): pl.pallas_call(body, out_shape=jax.ShapeDtypeStruct((tiles * LANES, PB),...]
where the time goes in v4:
time: 103 us; the launch traced here: 101 us
  Pallas kernels  98.9 us (96%)
  other arithmetic  1.54 us (1%)
    pallas_call x1, Pallas kernels, moved(): pl.pallas_call(gather_and_close, out_shape=[jax.ShapeDtypeStruct((8, 4, P...  50.5 us
    pallas_call x1, Pallas kernels, tile_of(): pl.pallas_call(body, out_shape=jax.ShapeDtypeStruct((tiles * LANES, PB),...  48.4 us

profile of v4, /device:TPU:1, one launch (start us, length us, event | category | flops | bytes accessed | tf_op | source)
XLA Modules:
  0.0 101.5 jit_solution(12450286163226168293)
XLA Ops:
  0.7 0.1 pad_add_fusion.base
  0.7 0.7 convert_bitcast_fusion
  1.4 0.3 dynamic_update_slice.3
  1.8 0.8 maximum_maximum_fusion.own
  2.5 50.5 %shard_map.37 = (f32[8,4,40,256]{3,2,1,0:T(8,128)S(1)}, f32[2,4,40,256]{3,2,1,0:T(8,128)S(1)}, f32[2,4,40,256]{3,2,1,0:T(8,128)S(1)}, f32[8,64,128]{2,1,0:T(8,128)S(1)}) custom-call(s32[1]{0:T(128)S(6)} %copy.5.pivot, f32[40,256]{1,0:T(8,128)S(1)} %maximum_maximum_fusion.own), custom_call_target="tpu_custom_call" | custom-call | tf_op jit(solution)/shard_map/pallas_call | solution.py:198
  53.1 48.4 %shard_map.38 = f32[1024,256]{1,0:T(8,128)} custom-call(s32[3]{0:T(128)S(1)} %pad_add_fusion.base, f32[8,4,40,256]{3,2,1,0:T(8,128)S(1)} %get-tuple-element.9.rb, f32[2,4,40,256]{3,2,1,0:T(8,128)S(1)} %get-tuple-element.10.cb, f32[2,4,40,256]{3,2,1,0:T(8,128)S(1)} %get-tuple-element.11.pb, f32[8,64,128]{2,1,0:T(8,128)S(1)} %get-tuple-element.12.fold), custom_call_target="tpu_custom_call" | custom-call | tf_op jit(solution)/shard_map/pallas_call | solution.py:438
  (2 shorter events, 0.0 us)

commit v5 on v4

--- a/solution.py
+++ b/solution.py
@@ -54,8 +54,8 @@
     pl.semaphore_wait(barrier, 17)
 
 
-def gather_and_close(pivot, own, rows, cols, pivots, closed, first, second, ka, wide, fold,
-                     npd, npa, wa, wb, own_sem, s1, r1, s2, r2, s3, r3, s4, r4,
+def gather_and_close(pivot, points, lists, closed, bt, ct, wt, own, staged, rows, cols, pivots,
+                     first, second, ka, wide, fold, npd, npa, ncd, nra, wa, wb, wb2, own_sem, s1, r1, s2, r2, s3, r3, s4, r4,
                      sc, rc, sz, rz, sy, ry, sp, rp, sf, rf):
     row, col, y, zh, core = place()
     m = zh * 2 + core
@@ -64,13 +64,21 @@
     mine = rows.at[y * 2 + core, zh]
     partner = (row, y * 8 + zh * 2 + 1 - core)
 
+    load = pltpu.make_async_copy(points, own.at[pl.ds(0, SHARE)], own_sem.at[3])
+    load.start()
+    staged[...] = jnp.zeros_like(staged)
+    staged[:K, :SHARE] = lists[...].astype(F32)
+    turned = pltpu.roll(staged[...], zh * SHARE, 1)
+    own[SHARE:, :LANES] = turned[:8]
+    own[SHARE:, LANES:] = turned[8:]
+    greet(row, col, y, m)
+    load.wait()
     kept = [
         pltpu.make_async_copy(own, mine, own_sem.at[0]),
         pltpu.make_async_copy(own, first.at[row], own_sem.at[1]),
     ]
     for copy in kept:
         copy.start()
-    greet(row, col, y, m)
 
     sent = []
     for d in range(1, 8):
@@ -129,16 +137,17 @@
     def _():
         out.start()
 
-    base = pivot[0] * PB
+    base, base_r, base_c = pivot[0] * PB, row * (4 * PB), col * PB
     norms_across(pivots, npa)
     norms_down(pivots, npd)
-    weigh(pivots, base, npd, pivots, base, npa, ka, wa, wb)
+    note_lists(pivots, base, pivots, base, wa, wb)
+    weigh(pivots, base, npd, pivots, base, npa, ka, wa, wb, 0, 1)
     spread(ka, wide)
     folded(wide, fold.at[0], 0, PB // FOLD)
     top = core * LANES
 
-    def square(turn, carry):
-        old, new = lax.rem(turn, 2), lax.rem(turn + 1, 2)
+    def square(turn, meanwhile):
+        old, new = turn % 2, (turn + 1) % 2
 
         def done(at, best):
             best = [reduced(b) for b in best]
@@ -155,57 +164,75 @@
         ours = fold.at[new, :, pl.ds(low, half)]
         theirs = fold.at[new, :, pl.ds(pl.multiple_of(half - low, half), half)]
         copy = send(ours, ours, sf.at[new], rf.at[new], partner)
+        meanwhile()
         arrival(theirs, sf.at[new], rf.at[new], partner)
         copy.wait_send()
-        return carry
-
-    lax.fori_loop(0, 1, square, 0)
-    for d in range(1, 4):
-        k = lax.rem(y + d, 4)
-        share = rows.at[k * 2 + core]
-        arrival(share, sy.at[d], ry.at[k], (row, k * 8 + m))
-        sent.append(send(share, share, sp.at[d], rp.at[k], partner))
-    lax.fori_loop(1, SQUARINGS + 1, square, 0)
+
+    def forward():
+        for d in range(1, 4):
+            k = lax.rem(y + d, 4)
+            share = rows.at[k * 2 + core]
+            arrival(share, sy.at[d], ry.at[k], (row, k * 8 + m))
+            sent.append(send(share, share, sp.at[d], rp.at[k], partner))
+        for d in range(1, 8):
+            k = lax.rem(m + d, 8)
+            slot = cols.at[lax.rem(k, 2), k // 2]
+            arrival(slot, sc.at[d], rc.at[k], (col // 4, lax.rem(col, 4) * 8 + k))
+
+        @pl.when(whole)
+        def _():
+            keep.wait()
+
+        @pl.when(jnp.logical_not(whole))
+        def _():
+            out.wait_send()
+            arrival(cols.at[core, zh], sc.at[0], rc.at[m], (col // 4, lax.rem(col, 4) * 8 + m))
+
+    def panel():
+        norms_down(cols, ncd)
+        note_lists(cols, base_c, pivots, base, wa, wb)
+        weigh(cols, base_c, ncd, pivots, base, npa, bt, wa, wb, 0, 1)
+
+    def row_weights():
+        for k in range(4):
+            arrival(rows.at[k * 2 + 1 - core], sp.at[k], rp.at[k], partner)
+        norms_across(rows, nra)
+        note_lists(pivots, base, rows, base_r, wa, wb2)
+        weigh(pivots, base, npd, rows, base_r, nra, ct, wa, wb2, 0, 4)
+
+    def tile_weights():
+        note_lists(cols, base_c, rows, base_r, wa, wb2)
+        weigh(cols, base_c, ncd, rows, base_r, nra, wt, wa, wb2, 0, 4)
+
+    square(0, forward)
+    square(1, panel)
+    square(2, row_weights)
+    square(3, tile_weights)
     closed[...] = fold[(SQUARINGS + 1) % 2]
-
-    for d in range(1, 8):
-        k = lax.rem(m + d, 8)
-        slot = cols.at[lax.rem(k, 2), k // 2]
-        arrival(slot, sc.at[d], rc.at[k], (col // 4, lax.rem(col, 4) * 8 + k))
-
-    @pl.when(whole)
-    def _():
-        keep.wait()
-
-    @pl.when(jnp.logical_not(whole))
-    def _():
-        out.wait_send()
-
-    for k in range(4):
-        arrival(rows.at[k * 2 + 1 - core], sp.at[k], rp.at[k], partner)
-
-    @pl.when(jnp.logical_not(whole))
-    def _():
-        arrival(cols.at[core, zh], sc.at[0], rc.at[m], (col // 4, lax.rem(col, 4) * 8 + m))
-
     for copy in sent:
         copy.wait_send()
 
 
-def moved(piece, pivot):
+def prepared(pivot, points, lists):
     sem = pltpu.SemaphoreType.DMA
     vmem = pl.BlockSpec(memory_space=pltpu.VMEM)
+    i32 = jnp.int32
     return pl.pallas_call(
         gather_and_close,
         out_shape=[
-            jax.ShapeDtypeStruct((8, 4, PIECE, PB), F32),
-            jax.ShapeDtypeStruct((2, 4, PIECE, PB), F32),
-            jax.ShapeDtypeStruct((2, 4, PIECE, PB), F32),
             jax.ShapeDtypeStruct((2 * FOLD, PB // FOLD, LANES), F32),
+            jax.ShapeDtypeStruct((2, PB, LANES), F32),
+            jax.ShapeDtypeStruct((8, PB, LANES), F32),
+            jax.ShapeDtypeStruct((8, PB, LANES), F32),
         ],
-        in_specs=[pl.BlockSpec(memory_space=pltpu.SMEM), vmem],
+        in_specs=[pl.BlockSpec(memory_space=pltpu.SMEM), vmem, vmem],
         out_specs=[vmem] * 4,
         scratch_shapes=[
+            pltpu.VMEM((PIECE, PB), F32),
+            pltpu.VMEM((16, LANES), F32),
+            pltpu.VMEM((8, 4, PIECE, PB), F32),
+            pltpu.VMEM((2, 4, PIECE, PB), F32),
+            pltpu.VMEM((2, 4, PIECE, PB), F32),
             pltpu.VMEM((8, PIECE, PB), F32),
             pltpu.VMEM((4, PIECE, PB), F32),
             pltpu.VMEM((2, PB, LANES), F32),
@@ -213,17 +240,20 @@
             pltpu.VMEM((2, 2 * FOLD, PB // FOLD, LANES), F32),
             pltpu.VMEM((PB, LANES), F32),
             pltpu.VMEM((2, 8, LANES), F32),
-            pltpu.VMEM((PB, LANES), jnp.int32),
-            pltpu.VMEM((2, 8, LANES), jnp.int32),
-            sem((3,)),
+            pltpu.VMEM((PB, LANES), F32),
+            pltpu.VMEM((8, 8, LANES), F32),
+            pltpu.VMEM((PB, LANES), i32),
+            pltpu.VMEM((2, 8, LANES), i32),
+            pltpu.VMEM((8, 8, LANES), i32),
+            sem((4,)),
             sem((8,)), sem((8,)), sem((4,)), sem((4,)), sem((4,)), sem((4,)), sem((1,)), sem((1,)),
             sem((8,)), sem((8,)), sem((4,)), sem((4,)), sem((4,)), sem((4,)),
             sem((4,)), sem((4,)), sem((2,)), sem((2,)),
         ],
         compiler_params=pltpu.CompilerParams(
-            collective_id=0, has_side_effects=True, vmem_limit_bytes=24 << 20
+            collective_id=0, has_side_effects=True, vmem_limit_bytes=32 << 20
         ),
-    )(pivot, piece)
+    )(pivot, points, lists)
 
 
 def dot(a, b, dims):
@@ -282,7 +312,7 @@
     )
 
 
-def weigh(down_of, base_a, norm_a, across_of, base_b, norm_b, out, wa, wb):
+def note_lists(down_of, base_a, across_of, base_b, wa, wb):
     tiles = across_of.shape[0]
     for tile in range(2):
         bits = bits_of(lists_of(down_of, tile), base_b, 4 * tiles)
@@ -294,40 +324,37 @@
         return carry
 
     lax.fori_loop(0, tiles, words, 0)
-    a = jnp.concatenate([points_of(down_of, 0), points_of(down_of, 1)], axis=0)
-
-    def products(t, carry):
-        b = jnp.concatenate([points_of(across_of, 2 * t), points_of(across_of, 2 * t + 1)], axis=0)
-        inner = dot(a, b, ((1,), (1,)))
-        out[2 * t] = inner[:, :LANES]
-        out[2 * t + 1] = inner[:, LANES:]
-        return carry
-
-    lax.fori_loop(0, tiles // 2, products, 0)
-
+
+
+def weigh(down_of, base_a, norm_a, across_of, base_b, norm_b, out, wa, wb, first, last):
     lane = lax.broadcasted_iota(jnp.int32, (32, LANES), 1)
     inside = lane & 31
     across = (lane // 32) * 64 + inside
     down = lax.broadcasted_iota(jnp.int32, (32, LANES), 0)
 
-    def group(n, carry):
-        t, g = n // 8, n % 8
-        rows = pl.ds(pl.multiple_of(g * 32, 32), 32)
-        word_a = (t // 2) * 8 + t % 2
-        word_b = (g % 4) * 2 + g // 4
-        squares = norm_a[rows, :] + jnp.tile(norm_b[t], (4, 1)) - 2.0 * out[t, rows, :]
-        squares = jnp.maximum(squares, 0.0)
-        length = squares * lax.rsqrt(jnp.maximum(squares, 1.2e-38))
-        listed = lanes_of(wa[rows, :], (lane // 32) * 2 + word_a)
-        listed = jnp.right_shift(listed, inside)
-        lists = jnp.tile(wb[t, pl.ds(word_b, 8, stride=0), :], (4, 1))
-        listed = listed | jnp.right_shift(lists, down)
-        weighted = jnp.where((listed & 1) == 1, length, far_weight * length)
-        same = (down - across) == (base_b - base_a + 32 * (word_a - word_b))
-        out[t, rows, :] = jnp.where(same, 0.0, weighted)
+    def pair(n, carry):
+        a = jnp.concatenate([points_of(down_of, 0), points_of(down_of, 1)], axis=0)
+        b = jnp.concatenate([points_of(across_of, 2 * n), points_of(across_of, 2 * n + 1)], axis=0)
+        inner = dot(a, b, ((1,), (1,)))
+        for g in range(8):
+            rows = slice(g * 32, g * 32 + 32)
+            word_b = (g % 4) * 2 + g // 4
+            for core in range(2):
+                t, word_a = 2 * n + core, n * 8 + core
+                part = inner[rows, core * LANES : (core + 1) * LANES]
+                squares = norm_a[rows, :] + jnp.tile(norm_b[t], (4, 1)) - 2.0 * part
+                squares = jnp.maximum(squares, 0.0)
+                length = squares * lax.rsqrt(jnp.maximum(squares, 1.2e-38))
+                listed = lanes_of(wa[rows, :], (lane // 32) * 2 + word_a)
+                listed = jnp.right_shift(listed, inside)
+                lists = jnp.tile(wb[t, pl.ds(word_b, 8, stride=0), :], (4, 1))
+                listed = listed | jnp.right_shift(lists, down)
+                weighted = jnp.where((listed & 1) == 1, length, far_weight * length)
+                same = (down - across) == (base_b - base_a + 32 * (word_a - word_b))
+                out[t, rows, :] = jnp.where(same, 0.0, weighted)
         return carry
 
-    lax.fori_loop(0, tiles * 8, group, 0)
+    lax.fori_loop(first, last, pair, 0)
 
 
 def min_plus(left, right, fold, done, rows, top, count):
@@ -397,14 +424,7 @@
     lax.fori_loop(0, PB // 32, chunk, 0)
 
 
-def body(base, rb, cb, pb, fold, o_ref, ct, bt, xt, wt, nra, npd, npa, ncd, wa, wb):
-    row_base, col_base, pivot_base = base[0], base[1], base[2]
-    norms_across(rb, nra)
-    norms_across(pb, npa)
-    norms_down(pb, npd)
-    norms_down(cb, ncd)
-    weigh(cb, col_base, ncd, pb, pivot_base, npa, bt, wa, wb)
-
+def body(fold, bt, ct, wt, o_ref, xt, ot):
     def done(at, best):
         best = [reduced(b) for b in best]
         for tile in range(2):
@@ -412,18 +432,16 @@
             xt[tile, at, :] = jnp.minimum(bt[tile, at, :], kept)
 
     min_plus(bt, fold, FOLD, done, 32, 0, PB)
-    weigh(pb, pivot_base, npd, rb, row_base, nra, ct, wa, wb)
-    weigh(cb, col_base, ncd, rb, row_base, nra, wt, wa, wb)
 
     def done(at, best):
         for tile in range(8):
-            wt[tile, at, :] = jnp.minimum(wt[tile, at, :], best[tile])
+            ot[tile, at, :] = jnp.minimum(wt[tile, at, :], best[tile])
 
     min_plus(xt, ct, 1, done, 32, 0, PB)
     for t in range(8):
         for n in range(2):
             parts = [
-                wt[t, (m % 2) * LANES + (m // 2) * 32 : (m % 2) * LANES + (m // 2) * 32 + 32, :]
+                ot[t, (m % 2) * LANES + (m // 2) * 32 : (m % 2) * LANES + (m // 2) * 32 + 32, :]
                 for m in range(4 * n, 4 * n + 4)
             ]
             flat = jnp.concatenate(parts, axis=0).T
@@ -432,39 +450,24 @@
                 o_ref[top : top + 32, n * LANES : (n + 1) * LANES] = flat[zh * 32 : zh * 32 + 32]
 
 
-def tile_of(base, rows, cols, pivots, closed):
+def tile_of(closed, bt, ct, wt):
     vmem = pl.BlockSpec(memory_space=pltpu.VMEM)
-    tiles = rows.shape[0]
+    tiles = ct.shape[0]
     return pl.pallas_call(
         body,
         out_shape=jax.ShapeDtypeStruct((tiles * LANES, PB), F32),
-        in_specs=[pl.BlockSpec(memory_space=pltpu.SMEM)] + [vmem] * 4,
+        in_specs=[vmem] * 4,
         out_specs=vmem,
         scratch_shapes=[
-            pltpu.VMEM((tiles, PB, LANES), F32),
-            pltpu.VMEM((2, PB, LANES), F32),
             pltpu.VMEM((2, PB, LANES), F32),
             pltpu.VMEM((tiles, PB, LANES), F32),
-            pltpu.VMEM((tiles, 8, LANES), F32),
-            pltpu.VMEM((PB, LANES), F32),
-            pltpu.VMEM((2, 8, LANES), F32),
-            pltpu.VMEM((PB, LANES), F32),
-            pltpu.VMEM((PB, LANES), jnp.int32),
-            pltpu.VMEM((tiles, 8, LANES), jnp.int32),
         ],
-        compiler_params=pltpu.CompilerParams(vmem_limit_bytes=40 << 20),
-    )(base, rows, cols, pivots, closed)
+        compiler_params=pltpu.CompilerParams(vmem_limit_bytes=24 << 20),
+    )(closed, bt, ct, wt)
 
 
 def local(features, neighbors, pivot):
-    row, col, y, zh, core = place()
-    lists = jnp.zeros((16, LANES), F32)
-    lists = lax.dynamic_update_slice(lists, neighbors.T.astype(F32), (0, zh * SHARE))
-    lists = jnp.concatenate([lists[:8], lists[8:]], axis=1)
-    piece = jnp.concatenate([features, lists], axis=0)
-    rows, cols, pivots, closed = moved(piece, pivot)
-    base = jnp.stack([row * 1024, col * PB, pivot[0] * PB]).astype(jnp.int32)
-    return tile_of(base, rows, cols, pivots, closed)
+    return tile_of(*prepared(pivot, features, neighbors.T))
 
 
 def solution(mesh):

time: 103 us -> 103 us (level)
  other arithmetic: 1.54 us -> 0 us
  local copies, waits for them, and re-layouts: 0.31 us -> 1.45 us
  Pallas kernels: 98.9 us -> 100 us
    pallas_call x1, Pallas kernels: 50.5 us -> 69.4 us  [prepared(): pl.pallas_call(gather_and_close, out_shape=[jax.ShapeDtypeStruct((2 * FOL...]
    pallas_call x1, Pallas kernels: 48.4 us -> 30.9 us  [tile_of(): pl.pallas_call(body, out_shape=jax.ShapeDtypeStruct((tiles * LANES, PB),...]
    unnamed x0 -> x4, local copies, waits for them, and re-layouts: none -> 1.45 us
where the time goes in v5:
time: 103 us; the launch traced here: 102 us
  Pallas kernels  100 us (97%)
  local copies, waits for them, and re-layouts  1.45 us (1%)
    pallas_call x1, Pallas kernels, prepared(): pl.pallas_call(gather_and_close, out_shape=[jax.ShapeDtypeStruct((2 * FOL...  69.4 us
    pallas_call x1, Pallas kernels, tile_of(): pl.pallas_call(body, out_shape=jax.ShapeDtypeStruct((tiles * LANES, PB),...  30.9 us

profile of v5, /device:TPU:1, one launch (start us, length us, event | category | flops | bytes accessed | tf_op | source)
XLA Modules:
  0.0 102.4 jit_solution(9743017230555258286)
XLA Ops:
  0.7 0.0 copy-start
  0.7 0.7 copy-done
  1.4 0.0 copy-start.1
  1.4 0.7 copy-done.1
  2.1 69.4 %shard_map.37 = (f32[8,64,128]{2,1,0:T(8,128)S(1)}, f32[2,256,128]{2,1,0:T(8,128)S(1)}, f32[8,256,128]{2,1,0:T(8,128)S(1)}, f32[8,256,128]{2,1,0:T(8,128)S(1)}) custom-call(s32[1]{0:T(128)S(6)} %copy.4.pivot, f32[32,256]{1,0:T(8,128)S(1)} %copy-done, s32[10,32]{1,0:T(8,128)S(1)} %bitcast.1), custom_call_target="tpu_custom_call" | custom-call | tf_op jit(solution)/shard_map/pallas_call | solution.py:220
  71.5 30.9 %shard_map.38 = f32[1024,256]{1,0:T(8,128)} custom-call(f32[8,64,128]{2,1,0:T(8,128)S(1)} %get-tuple-element.9.fold, f32[2,256,128]{2,1,0:T(8,128)S(1)} %get-tuple-element.10.bt, f32[8,256,128]{2,1,0:T(8,128)S(1)} %get-tuple-element.11.ct, f32[8,256,128]{2,1,0:T(8,128)S(1)} %get-tuple-element.12.wt), custom_call_target="tpu_custom_call" | custom-call | tf_op jit(solution)/shard_map/pallas_call | solution.py:456
Async XLA Ops:
  0.7 0.8 copy-start
  1.4 0.7 copy-start.1

commit v6 on v5

--- a/solution.py
+++ b/solution.py
@@ -40,16 +40,26 @@
     ).wait_recv()
 
 
+def beside(row, d):
+    x, z = FAR_FIRST[d]
+    return lax.rem(row // 4 + z, 2) * 4 + lax.rem(lax.rem(row, 4) + x, 4)
+
+
+FAR_FIRST = ((0, 0), (2, 1), (1, 1), (3, 1), (2, 0), (0, 1), (1, 0), (3, 0))
+RING = (2, 1, 3)
+
+
 def greet(row, col, y, m):
     barrier = pltpu.get_barrier_semaphore()
 
     def signal(to):
         pl.semaphore_signal(barrier, inc=1, device_id=to, device_id_type=MESH)
 
+    for d in (4, 3, 5, 2, 6, 1, 7):
+        signal((row, y * 8 + lax.rem(m + d, 8)))
     for d in range(1, 8):
-        signal((lax.rem(row + d, 8), col))
-        signal((row, y * 8 + lax.rem(m + d, 8)))
-    for d in range(1, 4):
+        signal((beside(row, d), col))
+    for d in RING:
         signal((row, lax.rem(y + d, 4) * 8 + m))
     pl.semaphore_wait(barrier, 17)
 
@@ -60,7 +70,6 @@
     row, col, y, zh, core = place()
     m = zh * 2 + core
     home = row * 4 + y
-    whole = home == col
     mine = rows.at[y * 2 + core, zh]
     partner = (row, y * 8 + zh * 2 + 1 - core)
 
@@ -82,58 +91,57 @@
 
     sent = []
     for d in range(1, 8):
-        to = (lax.rem(row + d, 8), col)
-        sent.append(send(own, first.at[row], s1.at[d], r1.at[row], to))
-    for d in range(1, 4):
+        sent.append(send(own, first.at[row], s1.at[d], r1.at[row], (beside(row, d), col)))
+    for d in RING:
         to = (row, y * 8 + lax.rem(zh + d, 4) * 2 + core)
         sent.append(send(own, mine, sz.at[d], rz.at[zh], to))
     for d in range(1, 8):
-        k = lax.rem(row + d, 8)
+        k = beside(row, d)
         arrival(first.at[k], s1.at[d], r1.at[k], (k, col))
     for copy in kept:
         copy.wait()
     second[y] = first[pivot[0] // 4]
-    for d in range(1, 4):
+    for d in RING:
         to = (row, lax.rem(y + d, 4) * 8 + m)
         sent.append(send(second.at[y], second.at[y], s2.at[d], r2.at[y], to))
-    for d in range(1, 4):
+    for d in RING:
         k = lax.rem(y + d, 4)
         arrival(second.at[k], s2.at[d], r2.at[k], (row, k * 8 + m))
     pivots[core, zh] = second[lax.rem(pivot[0], 4)]
     piece = pivots.at[core, zh]
-    for d in range(1, 4):
+    for d in RING:
         to = (row, y * 8 + lax.rem(zh + d, 4) * 2 + core)
         sent.append(send(piece, piece, s3.at[d], r3.at[zh], to))
 
-    for d in range(1, 4):
+    for d in RING:
         k = lax.rem(zh + d, 4)
         arrival(rows.at[y * 2 + core, k], sz.at[d], rz.at[k], (row, y * 8 + k * 2 + core))
     share = rows.at[y * 2 + core]
-    for d in range(1, 4):
+    for d in RING:
         to = (row, lax.rem(y + d, 4) * 8 + m)
         sent.append(send(share, share, sy.at[d], ry.at[y], to))
 
-    for d in range(1, 4):
+    for d in RING:
         k = lax.rem(zh + d, 4)
         arrival(pivots.at[core, k], s3.at[d], r3.at[k], (row, y * 8 + k * 2 + core))
     sent.append(send(pivots.at[core], pivots.at[core], s4.at[0], r4.at[0], partner))
     sent.append(send(share, share, sp.at[0], rp.at[y], partner))
     arrival(pivots.at[1 - core], s4.at[0], r4.at[0], partner)
 
-    for d in range(1, 8):
-        to = (lax.rem(row + d, 8), home)
-        sent.append(send(own, cols.at[core, zh], sc.at[d], rc.at[m], to))
+    stays = jnp.logical_and(home == col, row == m)
+    given = cols.at[core, zh]
+    taken = cols.at[lax.rem(row, 2), row // 2]
     out = pltpu.make_async_remote_copy(
-        src_ref=own, dst_ref=cols.at[core, zh], send_sem=sc.at[0], recv_sem=rc.at[m],
-        device_id=(row, home), device_id_type=MESH,
-    )
-    keep = pltpu.make_async_copy(own, cols.at[core, zh], own_sem.at[2])
-
-    @pl.when(whole)
+        src_ref=own, dst_ref=given, send_sem=sc.at[0], recv_sem=rc.at[8],
+        device_id=(m, home), device_id_type=MESH,
+    )
+    keep = pltpu.make_async_copy(own, given, own_sem.at[2])
+
+    @pl.when(stays)
     def _():
         keep.start()
 
-    @pl.when(jnp.logical_not(whole))
+    @pl.when(jnp.logical_not(stays))
     def _():
         out.start()
 
@@ -169,26 +177,28 @@
         copy.wait_send()
 
     def forward():
-        for d in range(1, 4):
+        for d in (1, 3, 2):
             k = lax.rem(y + d, 4)
             share = rows.at[k * 2 + core]
             arrival(share, sy.at[d], ry.at[k], (row, k * 8 + m))
             sent.append(send(share, share, sp.at[d], rp.at[k], partner))
-        for d in range(1, 8):
-            k = lax.rem(m + d, 8)
-            slot = cols.at[lax.rem(k, 2), k // 2]
-            arrival(slot, sc.at[d], rc.at[k], (col // 4, lax.rem(col, 4) * 8 + k))
-
-        @pl.when(whole)
+
+        @pl.when(stays)
         def _():
             keep.wait()
 
-        @pl.when(jnp.logical_not(whole))
+        @pl.when(jnp.logical_not(stays))
         def _():
             out.wait_send()
-            arrival(cols.at[core, zh], sc.at[0], rc.at[m], (col // 4, lax.rem(col, 4) * 8 + m))
+            arrival(taken, sc.at[0], rc.at[8], (col // 4, lax.rem(col, 4) * 8 + row))
+
+        for d in range(1, 8):
+            sent.append(send(taken, taken, sc.at[d], rc.at[row], (beside(row, d), col)))
 
     def panel():
+        for d in range(1, 8):
+            k = beside(row, d)
+            arrival(cols.at[lax.rem(k, 2), k // 2], sc.at[d], rc.at[k], (k, col))
         norms_down(cols, ncd)
         note_lists(cols, base_c, pivots, base, wa, wb)
         weigh(cols, base_c, ncd, pivots, base, npa, bt, wa, wb, 0, 1)
@@ -205,8 +215,8 @@
         weigh(cols, base_c, ncd, rows, base_r, nra, wt, wa, wb2, 0, 4)
 
     square(0, forward)
-    square(1, panel)
-    square(2, row_weights)
+    square(1, row_weights)
+    square(2, panel)
     square(3, tile_weights)
     closed[...] = fold[(SQUARINGS + 1) % 2]
     for copy in sent:
@@ -247,7 +257,7 @@
             pltpu.VMEM((8, 8, LANES), i32),
             sem((4,)),
             sem((8,)), sem((8,)), sem((4,)), sem((4,)), sem((4,)), sem((4,)), sem((1,)), sem((1,)),
-            sem((8,)), sem((8,)), sem((4,)), sem((4,)), sem((4,)), sem((4,)),
+            sem((8,)), sem((9,)), sem((4,)), sem((4,)), sem((4,)), sem((4,)),
             sem((4,)), sem((4,)), sem((2,)), sem((2,)),
         ],
         compiler_params=pltpu.CompilerParams(

time: 103 us -> 87.8 us (0.85)
  Pallas kernels: 100 us -> 85.5 us
    pallas_call x1, Pallas kernels: 69.4 us -> 54.6 us  [prepared(): pl.pallas_call(gather_and_close, out_shape=[jax.ShapeDtypeStruct((2 * FOL...]
where the time goes in v6:
time: 87.8 us; the launch traced here: 87.6 us
  Pallas kernels  85.5 us (97%)
  local copies, waits for them, and re-layouts  1.45 us (2%)
    pallas_call x1, Pallas kernels, prepared(): pl.pallas_call(gather_and_close, out_shape=[jax.ShapeDtypeStruct((2 * FOL...  54.6 us
    pallas_call x1, Pallas kernels, tile_of(): pl.pallas_call(body, out_shape=jax.ShapeDtypeStruct((tiles * LANES, PB),...  30.9 us

profile of v6, /device:TPU:1, one launch (start us, length us, event | category | flops | bytes accessed | tf_op | source)
XLA Modules:
  0.0 87.6 jit_solution(8672800340561948719)
XLA Ops:
  0.7 0.0 copy-start
  0.7 0.7 copy-done
  1.4 0.0 copy-start.1
  1.4 0.7 copy-done.1
  2.1 54.6 %shard_map.37 = (f32[8,64,128]{2,1,0:T(8,128)S(1)}, f32[2,256,128]{2,1,0:T(8,128)S(1)}, f32[8,256,128]{2,1,0:T(8,128)S(1)}, f32[8,256,128]{2,1,0:T(8,128)S(1)}) custom-call(s32[1]{0:T(128)S(6)} %copy.4.pivot, f32[32,256]{1,0:T(8,128)S(1)} %copy-done, s32[10,32]{1,0:T(8,128)S(1)} %bitcast.1), custom_call_target="tpu_custom_call" | custom-call | tf_op jit(solution)/shard_map/pallas_call | solution.py:230
  56.7 30.9 %shard_map.38 = f32[1024,256]{1,0:T(8,128)} custom-call(f32[8,64,128]{2,1,0:T(8,128)S(1)} %get-tuple-element.9.fold, f32[2,256,128]{2,1,0:T(8,128)S(1)} %get-tuple-element.10.bt, f32[8,256,128]{2,1,0:T(8,128)S(1)} %get-tuple-element.11.ct, f32[8,256,128]{2,1,0:T(8,128)S(1)} %get-tuple-element.12.wt), custom_call_target="tpu_custom_call" | custom-call | tf_op jit(solution)/shard_map/pallas_call | solution.py:466
Async XLA Ops:
  0.7 0.8 copy-start
  1.4 0.7 copy-start.1

commit v7 on v6

--- a/solution.py
+++ b/solution.py
@@ -61,57 +61,91 @@
         signal((beside(row, d), col))
     for d in RING:
         signal((row, lax.rem(y + d, 4) * 8 + m))
-    pl.semaphore_wait(barrier, 17)
-
-
-def gather_and_close(pivot, points, lists, closed, bt, ct, wt, own, staged, rows, cols, pivots,
-                     first, second, ka, wide, fold, npd, npa, ncd, nra, wa, wb, wb2, own_sem, s1, r1, s2, r2, s3, r3, s4, r4,
-                     sc, rc, sz, rz, sy, ry, sp, rp, sf, rf):
+    return barrier
+
+
+PARTS = (pl.ds(0, 24), pl.ds(24, 16))
+
+
+def gather_and_close(pivot, points, lists, closed, bt, ct, wt, own, listed, staged, rows, cols,
+                     pivots, first_a, first_b, second_a, second_b, ka, wide, fold,
+                     npd, npa, ncd, nra, wa, wb, wb2, own_sem,
+                     s1, r1, s2, r2, s3, r3, s4, r4, sc, rc, sz, rz, sy, ry, sp, rp, sf, rf):
     row, col, y, zh, core = place()
     m = zh * 2 + core
     home = row * 4 + y
     mine = rows.at[y * 2 + core, zh]
     partner = (row, y * 8 + zh * 2 + 1 - core)
-
-    load = pltpu.make_async_copy(points, own.at[pl.ds(0, SHARE)], own_sem.at[3])
-    load.start()
+    first, second = (first_a, first_b), (second_a, second_b)
+
+    load = [
+        pltpu.make_async_copy(lists, listed, own_sem.at[0]),
+        pltpu.make_async_copy(points, own.at[pl.ds(0, SHARE)], own_sem.at[1]),
+    ]
+    for copy in load:
+        copy.start()
+    barrier = greet(row, col, y, m)
     staged[...] = jnp.zeros_like(staged)
-    staged[:K, :SHARE] = lists[...].astype(F32)
+    load[0].wait()
+    staged[:K, :SHARE] = listed[...].astype(F32)
     turned = pltpu.roll(staged[...], zh * SHARE, 1)
     own[SHARE:, :LANES] = turned[:8]
     own[SHARE:, LANES:] = turned[8:]
-    greet(row, col, y, m)
-    load.wait()
+    load[1].wait()
+    pl.semaphore_wait(barrier, 17)
+
+    sent = []
+    for h, part in enumerate(PARTS):
+        for d in range(1, 8):
+            to = (beside(row, d), col)
+            sent.append(send(own.at[part], first[h].at[row], s1.at[h, d], r1.at[h, row], to))
     kept = [
-        pltpu.make_async_copy(own, mine, own_sem.at[0]),
-        pltpu.make_async_copy(own, first.at[row], own_sem.at[1]),
+        pltpu.make_async_copy(own.at[part], first[h].at[row], own_sem.at[2 + h])
+        for h, part in enumerate(PARTS)
     ]
+    kept.append(pltpu.make_async_copy(own, mine, own_sem.at[4]))
     for copy in kept:
         copy.start()
-
-    sent = []
-    for d in range(1, 8):
-        sent.append(send(own, first.at[row], s1.at[d], r1.at[row], (beside(row, d), col)))
     for d in RING:
         to = (row, y * 8 + lax.rem(zh + d, 4) * 2 + core)
         sent.append(send(own, mine, sz.at[d], rz.at[zh], to))
-    for d in range(1, 8):
-        k = beside(row, d)
-        arrival(first.at[k], s1.at[d], r1.at[k], (k, col))
     for copy in kept:
         copy.wait()
-    second[y] = first[pivot[0] // 4]
-    for d in RING:
-        to = (row, lax.rem(y + d, 4) * 8 + m)
-        sent.append(send(second.at[y], second.at[y], s2.at[d], r2.at[y], to))
-    for d in RING:
-        k = lax.rem(y + d, 4)
-        arrival(second.at[k], s2.at[d], r2.at[k], (row, k * 8 + m))
-    pivots[core, zh] = second[lax.rem(pivot[0], 4)]
-    piece = pivots.at[core, zh]
-    for d in RING:
-        to = (row, y * 8 + lax.rem(zh + d, 4) * 2 + core)
-        sent.append(send(piece, piece, s3.at[d], r3.at[zh], to))
+    for h in range(2):
+        for d in range(1, 8):
+            k = beside(row, d)
+            arrival(first[h].at[k], s1.at[h, d], r1.at[h, k], (k, col))
+        second[h][y] = first[h][pivot[0] // 4]
+        for d in RING:
+            to = (row, lax.rem(y + d, 4) * 8 + m)
+            slot = second[h].at[y]
+            sent.append(send(slot, slot, s2.at[h, d], r2.at[h, y], to))
+    for h, part in enumerate(PARTS):
+        for d in RING:
+            k = lax.rem(y + d, 4)
+            arrival(second[h].at[k], s2.at[h, d], r2.at[h, k], (row, k * 8 + m))
+        pivots[core, zh, part] = second[h][lax.rem(pivot[0], 4)]
+        piece = pivots.at[core, zh, part]
+        for d in RING:
+            to = (row, y * 8 + lax.rem(zh + d, 4) * 2 + core)
+            sent.append(send(piece, piece, s3.at[h, d], r3.at[h, zh], to))
+
+    stays = jnp.logical_and(home == col, row == m)
+    given = cols.at[core, zh]
+    taken = cols.at[lax.rem(row, 2), row // 2]
+    out = pltpu.make_async_remote_copy(
+        src_ref=own, dst_ref=given, send_sem=sc.at[0], recv_sem=rc.at[8],
+        device_id=(m, home), device_id_type=MESH,
+    )
+    keep = pltpu.make_async_copy(own, given, own_sem.at[5])
+
+    @pl.when(stays)
+    def _():
+        keep.start()
+
+    @pl.when(jnp.logical_not(stays))
+    def _():
+        out.start()
 
     for d in RING:
         k = lax.rem(zh + d, 4)
@@ -121,29 +155,16 @@
         to = (row, lax.rem(y + d, 4) * 8 + m)
         sent.append(send(share, share, sy.at[d], ry.at[y], to))
 
-    for d in RING:
-        k = lax.rem(zh + d, 4)
-        arrival(pivots.at[core, k], s3.at[d], r3.at[k], (row, y * 8 + k * 2 + core))
-    sent.append(send(pivots.at[core], pivots.at[core], s4.at[0], r4.at[0], partner))
+    for h, part in enumerate(PARTS):
+        for d in RING:
+            k = lax.rem(zh + d, 4)
+            slot = pivots.at[core, k, part]
+            arrival(slot, s3.at[h, d], r3.at[h, k], (row, y * 8 + k * 2 + core))
+        half = pivots.at[core, :, part]
+        sent.append(send(half, half, s4.at[h], r4.at[h], partner))
     sent.append(send(share, share, sp.at[0], rp.at[y], partner))
-    arrival(pivots.at[1 - core], s4.at[0], r4.at[0], partner)
-
-    stays = jnp.logical_and(home == col, row == m)
-    given = cols.at[core, zh]
-    taken = cols.at[lax.rem(row, 2), row // 2]
-    out = pltpu.make_async_remote_copy(
-        src_ref=own, dst_ref=given, send_sem=sc.at[0], recv_sem=rc.at[8],
-        device_id=(m, home), device_id_type=MESH,
-    )
-    keep = pltpu.make_async_copy(own, given, own_sem.at[2])
-
-    @pl.when(stays)
-    def _():
-        keep.start()
-
-    @pl.when(jnp.logical_not(stays))
-    def _():
-        out.start()
+    for h, part in enumerate(PARTS):
+        arrival(pivots.at[1 - core, :, part], s4.at[h], r4.at[h], partner)
 
     base, base_r, base_c = pivot[0] * PB, row * (4 * PB), col * PB
     norms_across(pivots, npa)
@@ -152,6 +173,18 @@
     weigh(pivots, base, npd, pivots, base, npa, ka, wa, wb, 0, 1)
     spread(ka, wide)
     folded(wide, fold.at[0], 0, PB // FOLD)
+    @pl.when(stays)
+    def _():
+        keep.wait()
+
+    @pl.when(jnp.logical_not(stays))
+    def _():
+        out.wait_send()
+        arrival(taken, sc.at[0], rc.at[8], (col // 4, lax.rem(col, 4) * 8 + row))
+
+    for d in range(1, 8):
+        sent.append(send(taken, taken, sc.at[d], rc.at[row], (beside(row, d), col)))
+
     top = core * LANES
 
     def square(turn, meanwhile):
@@ -165,7 +198,7 @@
                 part = gathered(best[FOLD * tile : FOLD * tile + FOLD])
                 ka[tile, at, :] = jnp.minimum(ka[tile, at, :], part)
 
-        min_plus(ka, fold.at[old], FOLD, done, 32, top, LANES)
+        min_plus(ka, fold.at[old], FOLD, done, 32, lambda t: top + 32 * t, 0, 4)
         half = LANES // FOLD
         low = pl.multiple_of(core * half, half)
         folded(wide.at[:, pl.ds(pl.multiple_of(top, LANES), LANES)], fold.at[new], low, half)
@@ -183,18 +216,6 @@
             arrival(share, sy.at[d], ry.at[k], (row, k * 8 + m))
             sent.append(send(share, share, sp.at[d], rp.at[k], partner))
 
-        @pl.when(stays)
-        def _():
-            keep.wait()
-
-        @pl.when(jnp.logical_not(stays))
-        def _():
-            out.wait_send()
-            arrival(taken, sc.at[0], rc.at[8], (col // 4, lax.rem(col, 4) * 8 + row))
-
-        for d in range(1, 8):
-            sent.append(send(taken, taken, sc.at[d], rc.at[row], (beside(row, d), col)))
-
     def panel():
         for d in range(1, 8):
             k = beside(row, d)
@@ -212,12 +233,19 @@
 
     def tile_weights():
         note_lists(cols, base_c, rows, base_r, wa, wb2)
-        weigh(cols, base_c, ncd, rows, base_r, nra, wt, wa, wb2, 0, 4)
-
-    square(0, forward)
+        weigh(cols, base_c, ncd, rows, base_r, nra, wt, wa, wb2, 0, 2)
+
+    def more_tile_weights():
+        weigh(cols, base_c, ncd, rows, base_r, nra, wt, wa, wb2, 2, 4)
+
+    def first_work():
+        forward()
+        panel()
+
+    square(0, first_work)
     square(1, row_weights)
-    square(2, panel)
-    square(3, tile_weights)
+    square(2, tile_weights)
+    square(3, more_tile_weights)
     closed[...] = fold[(SQUARINGS + 1) % 2]
     for copy in sent:
         copy.wait_send()
@@ -226,6 +254,7 @@
 def prepared(pivot, points, lists):
     sem = pltpu.SemaphoreType.DMA
     vmem = pl.BlockSpec(memory_space=pltpu.VMEM)
+    hbm = pl.BlockSpec(memory_space=pltpu.HBM)
     i32 = jnp.int32
     return pl.pallas_call(
         gather_and_close,
@@ -235,16 +264,19 @@
             jax.ShapeDtypeStruct((8, PB, LANES), F32),
             jax.ShapeDtypeStruct((8, PB, LANES), F32),
         ],
-        in_specs=[pl.BlockSpec(memory_space=pltpu.SMEM), vmem, vmem],
+        in_specs=[pl.BlockSpec(memory_space=pltpu.SMEM), hbm, hbm],
         out_specs=[vmem] * 4,
         scratch_shapes=[
             pltpu.VMEM((PIECE, PB), F32),
+            pltpu.VMEM((K, SHARE), i32),
             pltpu.VMEM((16, LANES), F32),
             pltpu.VMEM((8, 4, PIECE, PB), F32),
             pltpu.VMEM((2, 4, PIECE, PB), F32),
             pltpu.VMEM((2, 4, PIECE, PB), F32),
-            pltpu.VMEM((8, PIECE, PB), F32),
-            pltpu.VMEM((4, PIECE, PB), F32),
+            pltpu.VMEM((8, PARTS[0].size, PB), F32),
+            pltpu.VMEM((8, PARTS[1].size, PB), F32),
+            pltpu.VMEM((4, PARTS[0].size, PB), F32),
+            pltpu.VMEM((4, PARTS[1].size, PB), F32),
             pltpu.VMEM((2, PB, LANES), F32),
             pltpu.VMEM((2 * FOLD, PB, LANES), F32),
             pltpu.VMEM((2, 2 * FOLD, PB // FOLD, LANES), F32),
@@ -255,8 +287,9 @@
             pltpu.VMEM((PB, LANES), i32),
             pltpu.VMEM((2, 8, LANES), i32),
             pltpu.VMEM((8, 8, LANES), i32),
-            sem((4,)),
-            sem((8,)), sem((8,)), sem((4,)), sem((4,)), sem((4,)), sem((4,)), sem((1,)), sem((1,)),
+            sem((6,)),
+            sem((2, 8)), sem((2, 8)), sem((2, 4)), sem((2, 4)), sem((2, 4)), sem((2, 4)),
+            sem((2,)), sem((2,)),
             sem((8,)), sem((9,)), sem((4,)), sem((4,)), sem((4,)), sem((4,)),
             sem((4,)), sem((4,)), sem((2,)), sem((2,)),
         ],
@@ -367,7 +400,7 @@
     lax.fori_loop(first, last, pair, 0)
 
 
-def min_plus(left, right, fold, done, rows, top, count):
+def min_plus(left, right, fold, done, rows, start_of, first, last):
     tiles = right.shape[0]
     halves = left.shape[0]
     depth = right.shape[1] // halves
@@ -376,7 +409,7 @@
 
     def block(t, carry):
         def rows_of(s):
-            return pl.ds(pl.multiple_of(top + t * rows + 8 * s, 8), 8)
+            return pl.ds(pl.multiple_of(start_of(t) + 8 * s, 8), 8)
 
         def half(h, best):
             best = list(best)
@@ -396,7 +429,7 @@
             done(rows_of(s), [best[tile * subs + s] for tile in range(tiles)])
         return carry
 
-    lax.fori_loop(0, count // rows, block, 0)
+    lax.fori_loop(first, last, block, 0)
 
 
 def folded(wide, right, low, count):
@@ -441,13 +474,13 @@
             kept = gathered(best[FOLD * tile : FOLD * tile + FOLD])
             xt[tile, at, :] = jnp.minimum(bt[tile, at, :], kept)
 
-    min_plus(bt, fold, FOLD, done, 32, 0, PB)
+    min_plus(bt, fold, FOLD, done, 32, lambda t: 32 * t, 0, 8)
 
     def done(at, best):
         for tile in range(8):
             ot[tile, at, :] = jnp.minimum(wt[tile, at, :], best[tile])
 
-    min_plus(xt, ct, 1, done, 32, 0, PB)
+    min_plus(xt, ct, 1, done, 32, lambda t: 32 * t, 0, 8)
     for t in range(8):
         for n in range(2):
             parts = [
@@ -477,7 +510,9 @@
 
 
 def local(features, neighbors, pivot):
-    return tile_of(*prepared(pivot, features, neighbors.T))
+    features = pltpu.with_memory_space_constraint(features, pltpu.HBM)
+    lists = pltpu.with_memory_space_constraint(neighbors.T, pltpu.HBM)
+    return tile_of(*prepared(pivot, features, lists))
 
 
 def solution(mesh):

time: 87.8 us -> 85.9 us (0.978)
  local copies, waits for them, and re-layouts: 1.45 us -> 0 us
    pallas_call x1, Pallas kernels: 30.9 us -> 29.1 us  [tile_of(): pl.pallas_call(body, out_shape=jax.ShapeDtypeStruct((tiles * LANES, PB),...]
    unnamed x4 -> x0, local copies, waits for them, and re-layouts: 1.45 us -> none
    pallas_call x1, Pallas kernels: 54.6 us -> 56 us  [prepared(): pl.pallas_call(gather_and_close, out_shape=[jax.ShapeDtypeStruct((2 * FOL...]
where the time goes in v7:
time: 85.9 us; the launch traced here: 85.8 us
  Pallas kernels  85.1 us (99%)
    pallas_call x1, Pallas kernels, prepared(): pl.pallas_call(gather_and_close, out_shape=[jax.ShapeDtypeStruct((2 * FOL...  56 us
    pallas_call x1, Pallas kernels, tile_of(): pl.pallas_call(body, out_shape=jax.ShapeDtypeStruct((tiles * LANES, PB),...  29.1 us

profile of v7, /device:TPU:1, one launch (start us, length us, event | category | flops | bytes accessed | tf_op | source)
XLA Modules:
  0.0 85.8 jit_solution(12769067251431530503)
XLA Ops:
  0.7 56.0 %shard_map.37 = (f32[8,64,128]{2,1,0:T(8,128)S(1)}, f32[2,256,128]{2,1,0:T(8,128)S(1)}, f32[8,256,128]{2,1,0:T(8,128)S(1)}, f32[8,256,128]{2,1,0:T(8,128)S(1)}) custom-call(s32[1]{0:T(128)S(6)} %copy.4.pivot, f32[32,256]{1,0:T(8,128)} %points.1, s32[10,32]{1,0:T(8,128)} %bitcast.1), custom_call_target="tpu_custom_call" | custom-call | tf_op jit(solution)/shard_map/pallas_call | solution.py:259
  56.7 29.1 %shard_map.38 = f32[1024,256]{1,0:T(8,128)} custom-call(f32[8,64,128]{2,1,0:T(8,128)S(1)} %get-tuple-element.9.fold, f32[2,256,128]{2,1,0:T(8,128)S(1)} %get-tuple-element.10.bt, f32[8,256,128]{2,1,0:T(8,128)S(1)} %get-tuple-element.11.ct, f32[8,256,128]{2,1,0:T(8,128)S(1)} %get-tuple-element.12.wt), custom_call_target="tpu_custom_call" | custom-call | tf_op jit(solution)/shard_map/pallas_call | solution.py:499

commit v8 on v7

--- a/solution.py
+++ b/solution.py
@@ -139,14 +139,6 @@
     )
     keep = pltpu.make_async_copy(own, given, own_sem.at[5])
 
-    @pl.when(stays)
-    def _():
-        keep.start()
-
-    @pl.when(jnp.logical_not(stays))
-    def _():
-        out.start()
-
     for d in RING:
         k = lax.rem(zh + d, 4)
         arrival(rows.at[y * 2 + core, k], sz.at[d], rz.at[k], (row, y * 8 + k * 2 + core))
@@ -166,6 +158,14 @@
     for h, part in enumerate(PARTS):
         arrival(pivots.at[1 - core, :, part], s4.at[h], r4.at[h], partner)
 
+    @pl.when(stays)
+    def _():
+        keep.start()
+
+    @pl.when(jnp.logical_not(stays))
+    def _():
+        out.start()
+
     base, base_r, base_c = pivot[0] * PB, row * (4 * PB), col * PB
     norms_across(pivots, npa)
     norms_down(pivots, npd)
@@ -173,18 +173,6 @@
     weigh(pivots, base, npd, pivots, base, npa, ka, wa, wb, 0, 1)
     spread(ka, wide)
     folded(wide, fold.at[0], 0, PB // FOLD)
-    @pl.when(stays)
-    def _():
-        keep.wait()
-
-    @pl.when(jnp.logical_not(stays))
-    def _():
-        out.wait_send()
-        arrival(taken, sc.at[0], rc.at[8], (col // 4, lax.rem(col, 4) * 8 + row))
-
-    for d in range(1, 8):
-        sent.append(send(taken, taken, sc.at[d], rc.at[row], (beside(row, d), col)))
-
     top = core * LANES
 
     def square(turn, meanwhile):
@@ -216,6 +204,19 @@
             arrival(share, sy.at[d], ry.at[k], (row, k * 8 + m))
             sent.append(send(share, share, sp.at[d], rp.at[k], partner))
 
+    def relay():
+        @pl.when(stays)
+        def _():
+            keep.wait()
+
+        @pl.when(jnp.logical_not(stays))
+        def _():
+            out.wait_send()
+            arrival(taken, sc.at[0], rc.at[8], (col // 4, lax.rem(col, 4) * 8 + row))
+
+        for d in range(1, 8):
+            sent.append(send(taken, taken, sc.at[d], rc.at[row], (beside(row, d), col)))
+
     def panel():
         for d in range(1, 8):
             k = beside(row, d)
@@ -240,12 +241,16 @@
 
     def first_work():
         forward()
-        panel()
+        relay()
+
+    def last_work():
+        tile_weights()
+        more_tile_weights()
 
     square(0, first_work)
     square(1, row_weights)
-    square(2, tile_weights)
-    square(3, more_tile_weights)
+    square(2, panel)
+    square(3, last_work)
     closed[...] = fold[(SQUARINGS + 1) % 2]
     for copy in sent:
         copy.wait_send()

time: 85.9 us -> 84 us (0.978)
  Pallas kernels: 85.1 us -> 83.2 us
    pallas_call x1, Pallas kernels: 56 us -> 54.1 us  [prepared(): pl.pallas_call(gather_and_close, out_shape=[jax.ShapeDtypeStruct((2 * FOL...]
where the time goes in v8:
time: 84 us; the launch traced here: 83.9 us
  Pallas kernels  83.2 us (99%)
    pallas_call x1, Pallas kernels, prepared(): pl.pallas_call(gather_and_close, out_shape=[jax.ShapeDtypeStruct((2 * FOL...  54.1 us
    pallas_call x1, Pallas kernels, tile_of(): pl.pallas_call(body, out_shape=jax.ShapeDtypeStruct((tiles * LANES, PB),...  29.1 us

profile of v8, /device:TPU:1, one launch (start us, length us, event | category | flops | bytes accessed | tf_op | source)
XLA Modules:
  0.0 83.9 jit_solution(3424170284274355776)
XLA Ops:
  0.7 54.1 %shard_map.37 = (f32[8,64,128]{2,1,0:T(8,128)S(1)}, f32[2,256,128]{2,1,0:T(8,128)S(1)}, f32[8,256,128]{2,1,0:T(8,128)S(1)}, f32[8,256,128]{2,1,0:T(8,128)S(1)}) custom-call(s32[1]{0:T(128)S(6)} %copy.4.pivot, f32[32,256]{1,0:T(8,128)} %points.1, s32[10,32]{1,0:T(8,128)} %bitcast.1), custom_call_target="tpu_custom_call" | custom-call | tf_op jit(solution)/shard_map/pallas_call | solution.py:264
  54.8 29.1 %shard_map.38 = f32[1024,256]{1,0:T(8,128)} custom-call(f32[8,64,128]{2,1,0:T(8,128)S(1)} %get-tuple-element.9.fold, f32[2,256,128]{2,1,0:T(8,128)S(1)} %get-tuple-element.10.bt, f32[8,256,128]{2,1,0:T(8,128)S(1)} %get-tuple-element.11.ct, f32[8,256,128]{2,1,0:T(8,128)S(1)} %get-tuple-element.12.wt), custom_call_target="tpu_custom_call" | custom-call | tf_op jit(solution)/shard_map/pallas_call | solution.py:504

commit v9 on v8

--- a/solution.py
+++ b/solution.py
@@ -106,9 +106,6 @@
     kept.append(pltpu.make_async_copy(own, mine, own_sem.at[4]))
     for copy in kept:
         copy.start()
-    for d in RING:
-        to = (row, y * 8 + lax.rem(zh + d, 4) * 2 + core)
-        sent.append(send(own, mine, sz.at[d], rz.at[zh], to))
     for copy in kept:
         copy.wait()
     for h in range(2):
@@ -120,6 +117,9 @@
             to = (row, lax.rem(y + d, 4) * 8 + m)
             slot = second[h].at[y]
             sent.append(send(slot, slot, s2.at[h, d], r2.at[h, y], to))
+    for d in RING:
+        to = (row, y * 8 + lax.rem(zh + d, 4) * 2 + core)
+        sent.append(send(own, mine, sz.at[d], rz.at[zh], to))
     for h, part in enumerate(PARTS):
         for d in RING:
             k = lax.rem(y + d, 4)

time: 84 us -> 82.8 us (0.986)
  Pallas kernels: 83.2 us -> 82 us
    pallas_call x1, Pallas kernels: 54.1 us -> 52.9 us  [prepared(): pl.pallas_call(gather_and_close, out_shape=[jax.ShapeDtypeStruct((2 * FOL...]
where the time goes in v9:
time: 82.8 us; the launch traced here: 82.6 us
  Pallas kernels  82 us (99%)
    pallas_call x1, Pallas kernels, prepared(): pl.pallas_call(gather_and_close, out_shape=[jax.ShapeDtypeStruct((2 * FOL...  52.9 us
    pallas_call x1, Pallas kernels, tile_of(): pl.pallas_call(body, out_shape=jax.ShapeDtypeStruct((tiles * LANES, PB),...  29.1 us

profile of v9, /device:TPU:1, one launch (start us, length us, event | category | flops | bytes accessed | tf_op | source)
XLA Modules:
  0.0 82.6 jit_solution(7088461913949435432)
XLA Ops:
  0.7 52.9 %shard_map.37 = (f32[8,64,128]{2,1,0:T(8,128)S(1)}, f32[2,256,128]{2,1,0:T(8,128)S(1)}, f32[8,256,128]{2,1,0:T(8,128)S(1)}, f32[8,256,128]{2,1,0:T(8,128)S(1)}) custom-call(s32[1]{0:T(128)S(6)} %copy.4.pivot, f32[32,256]{1,0:T(8,128)} %points.1, s32[10,32]{1,0:T(8,128)} %bitcast.1), custom_call_target="tpu_custom_call" | custom-call | tf_op jit(solution)/shard_map/pallas_call | solution.py:264
  53.5 29.1 %shard_map.38 = f32[1024,256]{1,0:T(8,128)} custom-call(f32[8,64,128]{2,1,0:T(8,128)S(1)} %get-tuple-element.9.fold, f32[2,256,128]{2,1,0:T(8,128)S(1)} %get-tuple-element.10.bt, f32[8,256,128]{2,1,0:T(8,128)S(1)} %get-tuple-element.11.ct, f32[8,256,128]{2,1,0:T(8,128)S(1)} %get-tuple-element.12.wt), custom_call_target="tpu_custom_call" | custom-call | tf_op jit(solution)/shard_map/pallas_call | solution.py:504

commit v10 on v9

--- a/solution.py
+++ b/solution.py
@@ -64,7 +64,7 @@
     return barrier
 
 
-PARTS = (pl.ds(0, 24), pl.ds(24, 16))
+PARTS = (pl.ds(0, 16), pl.ds(16, 24))
 
 
 def gather_and_close(pivot, points, lists, closed, bt, ct, wt, own, listed, staged, rows, cols,

time: 82.8 us -> 83.3 us (level)
  no operation moved by 1% of the time
where the time goes in v10:
time: 83.3 us; the launch traced here: 83.2 us
  Pallas kernels  82.5 us (99%)
    pallas_call x1, Pallas kernels, prepared(): pl.pallas_call(gather_and_close, out_shape=[jax.ShapeDtypeStruct((2 * FOL...  53.4 us
    pallas_call x1, Pallas kernels, tile_of(): pl.pallas_call(body, out_shape=jax.ShapeDtypeStruct((tiles * LANES, PB),...  29.1 us

profile of v10, /device:TPU:1, one launch (start us, length us, event | category | flops | bytes accessed | tf_op | source)
XLA Modules:
  0.0 83.2 jit_solution(8662227816874693777)
XLA Ops:
  0.7 53.4 %shard_map.37 = (f32[8,64,128]{2,1,0:T(8,128)S(1)}, f32[2,256,128]{2,1,0:T(8,128)S(1)}, f32[8,256,128]{2,1,0:T(8,128)S(1)}, f32[8,256,128]{2,1,0:T(8,128)S(1)}) custom-call(s32[1]{0:T(128)S(6)} %copy.4.pivot, f32[32,256]{1,0:T(8,128)} %points.1, s32[10,32]{1,0:T(8,128)} %bitcast.1), custom_call_target="tpu_custom_call" | custom-call | tf_op jit(solution)/shard_map/pallas_call | solution.py:264
  54.1 29.1 %shard_map.38 = f32[1024,256]{1,0:T(8,128)} custom-call(f32[8,64,128]{2,1,0:T(8,128)S(1)} %get-tuple-element.9.fold, f32[2,256,128]{2,1,0:T(8,128)S(1)} %get-tuple-element.10.bt, f32[8,256,128]{2,1,0:T(8,128)S(1)} %get-tuple-element.11.ct, f32[8,256,128]{2,1,0:T(8,128)S(1)} %get-tuple-element.12.wt), custom_call_target="tpu_custom_call" | custom-call | tf_op jit(solution)/shard_map/pallas_call | solution.py:504
